TPU v7x, 512 devices: a whole 4x4x16 slice. The times are simulated.
512 devices in a mesh: gx: 32 (over y, x, core), vert: 16 (over z).
Axes of the slice: x: 4, y: 4, z: 16, core: 2. Of those that a mesh axis runs over, the one named last changes fastest.
Arguments:
- state: float32 [256, 16, 16384], P('gx', None, 'vert'), may hold values from -6 to 6
- macro: float32 [5, 256, 16], P(None, 'gx'), may hold values from -4 to 4
- relax_rate: float32 [256, 16], P('gx'), may hold values from 0.01 to 300, as said below
- velocity: float32 [3, 16384], P(None, 'vert'), may hold values from -2 to 4
- vel_sign: int32 [16384], P('vert'), may hold values from 0 to 1, as said below
- quad_weight: float32 [16384], P('vert'), may hold values from 0.5 to 2
- freestream: float32 [16, 16384], P(None, 'vert'), may hold values from -6 to 6
- wall_flag: int32 [16], replicated, may hold values 0 or 1
Outputs:
- new_state: float32 [256, 16, 16384], P('gx', None, 'vert')
- new_macro: float32 [5, 256, 16], P(None, 'gx')
Inputs may be any that keep to these rules, and one draw needn't show every extreme that they name: Each row of relax_rate varies from cell to cell. `vel_sign`: every aligned block of 1024 velocities holds both signs.
All inputs are finite; a program needn't handle non-finite values.
Results may differ from a plain program's by a relative error of at most 0.00013.
Values sent between devices are 32-bit elements; how exact they have to be, the bound alone decides.
No kernel may reach another device: no remote copies, remote signals or barrier semaphores. Data moves between devices by JAX's collectives and lax.ppermute only.
A program may use at most 64 MiB of HBM per device.

v0:
```python
import jax
import jax.numpy as jnp
from jax import lax
from jax.sharding import PartitionSpec as P

exact_mode = lax.Precision.HIGHEST


def prefix(value, axis, join, neutral, backward):
    count, mine = (lax.axis_size(axis), lax.axis_index(axis))
    pieces = jax.tree.map(lambda part: lax.all_gather(part, axis), value)
    if backward:
        pieces = jax.tree.map(lambda part: part[::-1], pieces)
        mine = count - 1 - mine
    total = jax.tree.map(
        lambda part, zero: jnp.full_like(part, 0) + jnp.asarray(zero, part.dtype), value, neutral
    )

    def turn(position, total):
        longer = join(total, jax.tree.map(lambda part: part[position], pieces))
        return jax.tree.map(lambda new, old: jnp.where(position < mine, new, old), longer, total)

    return lax.fori_loop(0, count - 1, turn, total)


def with_halo(cells, sides, width):
    for axis, dim in sides:
        count = lax.axis_size(axis)
        ends = count - 1
        head = lax.slice_in_dim(cells, 0, width, axis=dim)
        tail = lax.slice_in_dim(cells, cells.shape[dim] - width, cells.shape[dim], axis=dim)
        cells = jnp.concatenate(
            [
                lax.ppermute(tail, axis, [(i, (i + 1) % count) for i in range(ends)]),
                cells,
                lax.ppermute(head, axis, [((i + 1) % count, i) for i in range(ends)]),
            ],
            axis=dim,
        )
    return cells


def basis_sets(velocity, vel_sign, quad_weight, groups):
    magnitude = velocity[0]
    along_x = jnp.where(vel_sign == 1, magnitude, -magnitude)
    along_y = velocity[1]
    along_z = velocity[2]
    square = along_x * along_x + along_y * along_y + along_z * along_z
    ones_row = jnp.ones_like(along_x)
    equil_basis = jnp.stack([ones_row, 2.0 * along_x, 2.0 * along_y, 2.0 * along_z, square - 1.5])
    weights = quad_weight / (quad_weight.shape[0] * groups)
    heat_factor = 0.2 * (square - 2.5)
    moment_rows = jnp.stack(
        [
            ones_row,
            along_x,
            along_y,
            along_z,
            2.0 / 3.0 * square - 1.0,
            2.0 * along_x * along_y,
            2.0 * along_x * along_z,
            2.0 * along_y * along_z,
            2.0 * (along_x * along_x - square / 3.0),
            2.0 * (along_y * along_y - square / 3.0),
            heat_factor * along_x,
            heat_factor * along_y,
            heat_factor * along_z,
        ]
    )
    outflux = jnp.where(vel_sign == 0, weights * magnitude, 0.0)
    influx = jnp.where(vel_sign == 1, weights * magnitude, 0.0)
    return (magnitude, equil_basis, moment_rows * weights, outflux, influx)


def compose(earlier, latter):
    return (latter[0] * earlier[0], latter[0] * earlier[1] + latter[1])


def march_zero(decay, driven, reverse):

    def advance_cell(carried, pieces):
        zero_run = pieces[0] * carried[0] + pieces[1]
        product = pieces[0] * carried[1]
        return ((zero_run, product), (zero_run, product))

    initial = (jnp.zeros_like(driven[0]), jnp.ones_like(driven[0]))
    _, (zero_runs, products) = lax.scan(advance_cell, initial, (decay, driven), reverse=reverse)
    return (zero_runs, products)


def advance(padded, relax_cells):
    conserved = padded[:5]
    flow_x = jnp.stack(
        [
            padded[1],
            padded[0] + padded[4] + padded[8],
            padded[5],
            padded[6],
            2.0 / 3.0 * (padded[1] + padded[10]),
        ]
    )
    flow_y = jnp.stack(
        [
            padded[2],
            padded[5],
            padded[0] + padded[4] + padded[9],
            padded[7],
            2.0 / 3.0 * (padded[2] + padded[11]),
        ]
    )
    centre = conserved[:, 1:-1, 1:-1]
    laplace = (
        conserved[:, 2:, 1:-1]
        + conserved[:, :-2, 1:-1]
        + conserved[:, 1:-1, 2:]
        + conserved[:, 1:-1, :-2]
        - 4.0 * centre
    )
    divergence = (
        flow_x[:, 2:, 1:-1] - flow_x[:, :-2, 1:-1] + flow_y[:, 1:-1, 2:] - flow_y[:, 1:-1, :-2]
    )
    diffusivity = 0.2 / (1.0 + relax_cells)
    return (centre + diffusivity * laplace - 0.25 * divergence, centre)


def local(state, macro, relax_rate, velocity, vel_sign, quad_weight, freestream, wall_flag):
    cells_x = state.shape[0]
    cells_y = state.shape[1]
    vel_count = state.shape[2]
    slab_count = lax.axis_size("gx")
    slab_index = lax.axis_index("gx")
    magnitude, equil_basis, moment_basis, outflux, influx = basis_sets(
        velocity, vel_sign, quad_weight, lax.axis_size("vert")
    )
    courant = cells_x * slab_count * magnitude
    relax_cell = relax_rate[:, :, None]
    flat_macro = macro.reshape(macro.shape[0], cells_x * cells_y)
    equil_state = jnp.einsum("kc,kv->cv", flat_macro, equil_basis, precision=exact_mode).reshape(
        cells_x, cells_y, vel_count
    )
    source = state + relax_cell * equil_state
    wall_mask = wall_flag[:, None] == 1
    wall_in = jnp.sum(influx) / slab_count
    divisor = 1.0 + courant + relax_cell
    decay = courant / divisor
    driven = source / divisor
    back_runs, back_products = march_zero(decay, driven, True)
    fore_runs, fore_products = march_zero(decay, driven, False)
    ones_plane = jnp.ones((cells_y, vel_count), jnp.float32)
    zero_plane = jnp.zeros((cells_y, vel_count), jnp.float32)
    back_maps = prefix(
        (back_products[0], back_runs[0]), "gx", compose, (ones_plane, zero_plane), True
    )
    entry_back = back_maps[0] * freestream + back_maps[1]
    back = back_products * entry_back + back_runs
    at_anchor = slab_index == 0
    wall_out = jnp.where(at_anchor, jnp.dot(back[0], outflux, precision=exact_mode), 0.0)
    wall_out, wall_in = lax.psum((wall_out, wall_in), ("gx", "vert"))
    rho_wall = wall_out / wall_in
    inflow_left = jnp.where(wall_mask, rho_wall[:, None], freestream)
    fore_maps = prefix(
        (fore_products[-1], fore_runs[-1]), "gx", compose, (ones_plane, zero_plane), False
    )
    entry_fore = fore_maps[0] * inflow_left + fore_maps[1]
    fore = fore_products * entry_fore + fore_runs
    kinetic = jnp.where(vel_sign == 1, fore, back)
    flattened = kinetic.reshape(cells_x * cells_y, vel_count)
    partial_value = jnp.einsum("cv,kv->kc", flattened, moment_basis, precision=exact_mode).reshape(
        13, cells_x, cells_y
    )
    moments = lax.psum(partial_value, "vert")
    padded = with_halo(moments, (("gx", 1),), 1)
    padded = jnp.concatenate([padded[:, :, -1:], padded, padded[:, :, :1]], axis=2)
    updated, centre = advance(padded, relax_rate)
    change = updated - centre
    flat_change = change.reshape(change.shape[0], cells_x * cells_y)
    correction = jnp.einsum("kc,kv->cv", flat_change, equil_basis, precision=exact_mode).reshape(
        cells_x, cells_y, vel_count
    )
    return (kinetic + correction, updated)


def solution(mesh):
    return jax.shard_map(
        local,
        mesh=mesh,
        in_specs=(
            P("gx", None, "vert"),
            P(None, "gx", None),
            P("gx", None),
            P(None, "vert"),
            P("vert"),
            P("vert"),
            P(None, "vert"),
            P(),
        ),
        out_specs=(P("gx", None, "vert"), P(None, "gx", None)),
        check_vma=False,
    )
```

profile of v0, /device:TPU:7, one launch (start us, length us, event | category | flops | bytes accessed | tf_op | source)
XLA Modules:
  0.0 472.6 jit_solution(17301780224435400815)
XLA Ops:
  9.6 1.9 select_reduce_fusion
  12.1 1.2 add_divide_fusion
  19.7 58.5 %all-gather.9.cloned.1.call-done = f32[32,16,1024]{2,1,0:T(8,128)} async-done(((f32[1,16,1024]{2,1,0:T(8,128)}), f32[32,16,1024]{2,1,0:T(8,128)}) %all-gather.9.cloned.1.call-update) | async-done | bytes 2097168 | tf_op jit(solution)/shard_map/all_gather | solution.py:11
  78.2 1.7 rev.6
  79.9 59.8 %all-gather.11.cloned.1.call-done = f32[32,16,1024]{2,1,0:T(8,128)} async-done(((f32[1,16,1024]{2,1,0:T(8,128)}), f32[32,16,1024]{2,1,0:T(8,128)}) %all-gather.11.cloned.1.call-update) | async-done | bytes 2097168 | tf_op jit(solution)/shard_map/all_gather | solution.py:11
  139.6 3.2 rev.7
  142.9 28.3 %while.71 = (s32[]{:T(128)}, f32[16,1024]{1,0:T(8,128)S(1)}, f32[16,1024]{1,0:T(8,128)S(1)}, s32[]{:T(128)}, f32[32,16,1024]{2,1,0:T(8,128)S(1)}, /*index=5*/f32[32,16,1024]{2,1,0:T(8,128)}, s32[]{:T(128)}, s32[]{:T(128)}) while((s32[]{:T(128)}, f32[16,1024]{1,0:T(8,128)S(1)}, f32[16,1024]{1,0:T(8,128)S(1)}, s32[]{:T(128)}, ...), condition=%wide.region_7.8_spmd.clone, body=%wide.region_6.7_spmd.clone.sunk | while | flops 114692 | bytes 393325 | solution.py:23
  172.4 28.8 %all-gather.5.cloned.1.call-done = f32[32,16,1024]{2,1,0:T(8,128)} async-done(((f32[1,16,1024]{2,1,0:T(8,128)}), f32[32,16,1024]{2,1,0:T(8,128)}) %all-gather.5.cloned.1.call-update) | async-done | bytes 2097168 | tf_op jit(solution)/shard_map/all_gather | solution.py:11
  201.2 61.3 %all-gather.7.cloned.1.call-done = f32[32,16,1024]{2,1,0:T(8,128)} async-done(((f32[1,16,1024]{2,1,0:T(8,128)}), f32[32,16,1024]{2,1,0:T(8,128)}) %all-gather.7.cloned.1.call-update) | async-done | bytes 2097168 | tf_op jit(solution)/shard_map/all_gather | solution.py:11
  262.6 29.2 %while.70 = (s32[]{:T(128)}, f32[16,1024]{1,0:T(8,128)S(1)}, f32[16,1024]{1,0:T(8,128)S(1)}, s32[]{:T(128)}, f32[32,16,1024]{2,1,0:T(8,128)}, /*index=5*/f32[32,16,1024]{2,1,0:T(8,128)}, s32[]{:T(128)}, s32[]{:T(128)}) while((s32[]{:T(128)}, f32[16,1024]{1,0:T(8,128)S(1)}, f32[16,1024]{1,0:T(8,128)S(1)}, s32[]{:T(128)}, ...), condition=%wide.region_3.4_spmd.clone, body=%wide.region_2.3_spmd.clone.sunk | while | flops 114692 | bytes 393325 | solution.py:23
  262.6 0.9 fusion.39
  263.5 0.9 fusion.39
  264.4 0.9 fusion.39
  265.4 0.9 fusion.39
  266.3 0.9 fusion.39
  267.3 0.9 fusion.39
  268.2 0.9 fusion.39
  269.2 0.9 fusion.39
  270.1 0.9 fusion.39
  271.1 0.9 fusion.39
  272.0 0.9 fusion.39
  272.9 0.9 fusion.39
  273.9 0.9 fusion.39
  274.8 0.9 fusion.39
  275.8 0.9 fusion.39
  276.7 0.9 fusion.39
  277.7 0.9 fusion.39
  278.6 0.9 fusion.39
  279.6 0.9 fusion.39
  280.5 0.9 fusion.39
  281.4 0.9 fusion.39
  282.4 0.9 fusion.39
  283.3 0.9 fusion.39
  284.3 0.9 fusion.39
  285.2 0.9 fusion.39
  286.2 0.9 fusion.39
  287.1 0.9 fusion.39
  288.0 0.9 fusion.39
  289.0 0.9 fusion.39
  289.9 0.9 fusion.39
  290.9 0.9 fusion.39
  291.8 103.7 %all-reduce = (f32[16]{0:T(128)S(1)}, f32[]{:T(128)}) all-reduce(f32[16]{0:T(128)S(1)} %fusion.2, f32[]{:T(128)S(6)} %div.41), channel_id=1, replica_groups=mesh['gx'=32,'vert'=16] {'gx','vert'}, use_global_device_ids=true, to_apply=%region_8.9 | all-reduce | flops 17 | bytes 136 | tf_op jit(solution)/shard_map/psum | solution.py:158
  396.4 1.9 fusion.3
  398.4 40.2 %psum.23 = f32[13,8,16]{2,0,1:T(8,128)S(1)} all-reduce(f32[13,8,16]{2,0,1:T(8,128)S(1)} %fusion.3), channel_id=1, replica_groups=mesh['gx'=32,'vert'=16] {'vert'}, use_global_device_ids=true, to_apply=%region_11.12 | all-reduce | flops 1664 | bytes 13312 | tf_op jit(solution)/shard_map/psum | solution.py:171
  438.6 17.3 %collective-permute-start.1 = (f32[13,1,16]{2,0,1:T(8,128)S(1)}, f32[13,1,16]{2,0,1:T(8,128)S(1)}, u32[]{:S(2)}, u32[]{:S(2)}) collective-permute-start(f32[13,1,16]{2,0,1:T(8,128)S(1)} %get-tuple-element.544), channel_id=1, source_target_pairs={{0,16},{16,32},{32,48},{48,64},{64,80},{80,96},{96,112},{112,128},... | collective-permute-start | bytes 2504 | tf_op jit(solution)/shard_map/ppermute | solution.py:34
  455.9 1.9 collective-permute-start
  457.9 5.1 %collective-permute-done = f32[13,1,16]{2,0,1:T(8,128)S(1)} collective-permute-done((f32[13,1,16]{2,0,1:T(8,128)S(1)}, f32[13,1,16]{2,0,1:T(8,128)S(1)}, u32[]{:S(2)}, u32[]{:S(2)}) %collective-permute-start) | collective-permute-done | bytes 864 | tf_op jit(solution)/shard_map/ppermute | solution.py:36
  464.0 1.5 convolution_add_fusion
  (127 shorter events, 40.4 us)
Async XLA Ops:
  7.2 71.0 %all-gather.9.cloned.1.call-start = ((), (), s32[]{:S(2)}) async-start(), calls=%async_computation.2 | async-start | bytes 2162688 | tf_op jit(solution)/shard_map/all_gather | solution.py:11
  9.6 4.0 copy-start.7
  14.7 125.0 %all-gather.11.cloned.1.call-start = ((), (), s32[]{:S(2)}) async-start(), calls=%async_computation.3 | async-start | bytes 2162688 | tf_op jit(solution)/shard_map/all_gather | solution.py:11
  15.4 185.8 %all-gather.5.cloned.1.call-start = ((), (), s32[]{:S(2)}) async-start(), calls=%async_computation | async-start | bytes 2162688 | tf_op jit(solution)/shard_map/all_gather | solution.py:11
  15.5 2.1 copy-start.5
  15.5 2.2 copy-start.10
  16.2 3.5 copy-start
  16.2 3.5 copy-start.2
  16.9 245.7 %all-gather.7.cloned.1.call-start = ((), (), s32[]{:S(2)}) async-start(), calls=%async_computation.1 | async-start | bytes 2162688 | tf_op jit(solution)/shard_map/all_gather | solution.py:11
  171.2 225.0 %copy-start.4 = (f32[16,1024]{1,0:T(8,128)S(1)}, f32[16,1024]{1,0:T(8,128)}, u32[]{:S(2)}) copy-start(f32[16,1024]{1,0:T(8,128)} %param.22) | copy-start | bytes 196612
  171.2 225.0 %copy-start.9 = (pred[16]{0:T(512)(128)(4,1)S(1)}, pred[16]{0:T(512)(128)(4,1)}, u32[]{:S(2)}) copy-start(pred[16]{0:T(512)(128)(4,1)} %broadcast_compare_fusion.1) | copy-start | bytes 52
  172.1 224.2 %copy-start.1 = (f32[8,16,1024]{2,1,0:T(8,128)S(1)}, f32[8,16,1024]{2,1,0:T(8,128)}, u32[]{:S(2)}) copy-start(f32[8,16,1024]{2,1,0:T(8,128)} %copy-done) | copy-start | bytes 1572868
  172.1 224.2 %copy-start.3 = (f32[8,16,1024]{2,1,0:T(8,128)S(1)}, f32[8,16,1024]{2,1,0:T(8,128)}, u32[]{:S(2)}) copy-start(f32[8,16,1024]{2,1,0:T(8,128)} %copy-done.2) | copy-start | bytes 1572868
  172.1 224.2 %copy-start.8 = (pred[1024]{0:T(1024)(128)(4,1)S(1)}, pred[1024]{0:T(1024)(128)(4,1)}, u32[]{:S(2)}) copy-start(pred[1024]{0:T(1024)(128)(4,1)} %copy-done.7) | copy-start | bytes 3076
  291.8 164.1 %copy-start.6 = (f32[8,16]{1,0:T(8,128)S(1)}, f32[8,16]{1,0:T(8,128)}, u32[]{:S(2)}) copy-start(f32[8,16]{1,0:T(8,128)} %param.18) | copy-start | bytes 1540
  438.6 19.3 %collective-permute-start.1 = (f32[13,1,16]{2,0,1:T(8,128)S(1)}, f32[13,1,16]{2,0,1:T(8,128)S(1)}, u32[]{:S(2)}, u32[]{:S(2)}) collective-permute-start(f32[13,1,16]{2,0,1:T(8,128)S(1)} %get-tuple-element.544), channel_id=1, source_target_pairs={{0,16},{16,32},{32,48},{48,64},{64,80},{80,96},{96,112},{112,128},... | collective-permute-start | bytes 2504 | tf_op jit(solution)/shard_map/ppermute | solution.py:34
  455.9 7.1 %collective-permute-start = (f32[13,1,16]{2,0,1:T(8,128)S(1)}, f32[13,1,16]{2,0,1:T(8,128)S(1)}, u32[]{:S(2)}, u32[]{:S(2)}) collective-permute-start(f32[13,1,16]{2,0,1:T(8,128)S(1)} %get-tuple-element.543), channel_id=1, source_target_pairs={{16,0},{32,16},{48,32},{64,48},{80,64},{96,80},{112,96},{128,112},... | collective-permute-start | bytes 2504 | tf_op jit(solution)/shard_map/ppermute | solution.py:36
Sparse Core Ops, SparseCore 0:
  14.8 63.3 all-gather.8
  81.3 58.3 all-gather.10
  142.8 58.3 all-gather.4
  204.2 58.3 all-gather.6
where the time goes:
time: 476 us; the launch traced here: 473 us
  waiting for transfers between devices  214 us (45%)
  blocking collectives  144 us (30%)
  other arithmetic  64.6 us (14%)
  starting transfers between devices  19.4 us (4%)
  between operations  14.8 us (3%)
  local copies, waits for them, and re-layouts  10.4 us (2%)
    all_gather x4, waiting for transfers between devices, prefix(): pieces = jax.tree.map(lambda part: lax.all_gather(part, axis), value)  208 us
    psum x1, blocking collectives, local(): wall_out, wall_in = lax.psum((wall_out, wall_in), ('gx', 'vert'))  104 us
    select_n x62, other arithmetic, turn(): jnp.where(position < mine, new, old)  56.1 us
    psum x1, blocking collectives, local(): moments = lax.psum(partial_value, 'vert')  40.2 us
    ppermute x1, starting transfers between devices, with_halo(): lax.ppermute(tail, axis, [(i, (i + 1) % count) for i in range(ends)])  17.3 us
  transfers between devices with their start and end apart: 6, of which 5 were waited for; matrix products, arithmetic and copies ran while one was open for 8% of the time, Pallas kernels for 0%

commit v1 on v0

v1 whole, which is shorter than its diff:
```python
import jax
import jax.numpy as jnp
from jax import lax
from jax.experimental import pallas as pl
from jax.experimental.pallas import tpu as pltpu
from jax.sharding import PartitionSpec as P

LANES = 128
QUAD = 4
SENT_ROWS = 32
INTERPRET = False


def signed_velocity(velocity_ref, sign_ref, lanes):
    magnitude = velocity_ref[0:1, lanes]
    positive = sign_ref[0:1, lanes] == 1
    along_x = jnp.where(positive, magnitude, -magnitude)
    along_y = velocity_ref[1:2, lanes]
    along_z = velocity_ref[2:3, lanes]
    square = along_x * along_x + along_y * along_y + along_z * along_z
    return magnitude, positive, along_x, along_y, along_z, square


def maps_kernel(
    total_cells,
    state_ref,
    macro_ref,
    relax_ref,
    velocity_ref,
    sign_ref,
    free_ref,
    wall_ref,
    reach_ref,
    run_ref,
    sent_ref,
    side_ref,
    pad_ref,
    spread_ref,
):
    fields, cells_x, cells_y = macro_ref.shape
    tiles = state_ref.shape[2] // LANES
    pad_ref[...] = jnp.zeros_like(pad_ref)
    for k in range(fields):
        pad_ref[k * cells_x : (k + 1) * cells_x, 0:cells_y] = macro_ref[k]
    base_row = fields * cells_x
    pad_ref[base_row : base_row + cells_x, 0:cells_y] = relax_ref[...]
    wall_row = base_row + cells_x
    pad_ref[wall_row : wall_row + 1, 0:cells_y] = (wall_ref[...] == 1).astype(jnp.float32)
    columns = pad_ref[...].T
    for c in range(wall_row + 1):
        spread_ref[c] = jnp.broadcast_to(columns[0:cells_y, c : c + 1], (cells_y, LANES))
    for tile in range(tiles):
        lanes = slice(tile * LANES, (tile + 1) * LANES)
        magnitude, positive, along_x, along_y, along_z, square = signed_velocity(
            velocity_ref, sign_ref, lanes
        )
        courant = total_cells * magnitude
        base = 1.0 + courant
        basis = [2.0 * along_x, 2.0 * along_y, 2.0 * along_z, square - 1.5]
        for half in range(cells_y // 8):
            rows = slice(half * 8, half * 8 + 8)
            forward = jnp.broadcast_to(positive, (8, LANES))
            decay = []
            driven = []
            for x in range(cells_x):
                relax = spread_ref[base_row + x, rows]
                equil = spread_ref[x, rows]
                for k in range(1, fields):
                    equil = equil + spread_ref[k * cells_x + x, rows] * basis[k - 1]
                inverse = 1.0 / (base + relax)
                decay.append(courant * inverse)
                driven.append((state_ref[x, rows, lanes] + relax * equil) * inverse)
            last = cells_x - 1
            steps = [jnp.where(forward, decay[t], decay[last - t]) for t in range(cells_x)]
            gains = [jnp.where(forward, driven[t], driven[last - t]) for t in range(cells_x)]
            products = [steps[0]]
            runs = [gains[0]]
            for t in range(1, cells_x):
                products.append(steps[t] * products[-1])
                runs.append(steps[t] * runs[-1] + gains[t])
            for x in range(cells_x):
                reach_ref[x, rows, lanes] = jnp.where(forward, products[x], products[last - x])
                run_ref[x, rows, lanes] = jnp.where(forward, runs[x], runs[last - x])
            wall = spread_ref[wall_row, rows] > 0.5
            free = free_ref[rows, lanes]
            diffuse = jnp.logical_and(forward, wall)
            fixed = jnp.where(diffuse, 0.0, free)
            unit = jnp.where(diffuse, 1.0, 0.0)
            direction = jnp.where(forward, 1.0, 0.0)
            for part in range(8 // QUAD):
                owner = (half * (8 // QUAD) + part) * tiles + tile
                quad = slice(part * QUAD, (part + 1) * QUAD)
                for slot, value in enumerate((products[last], runs[last], steps[0], gains[0])):
                    sent_ref[owner, slot * QUAD : (slot + 1) * QUAD, :] = value[quad]
                for slot, value in enumerate((fixed, unit, direction)):
                    side_ref[owner, slot * QUAD : (slot + 1) * QUAD, :] = value[quad]


def scan_kernel(maps_ref, side_ref, sent_ref, entry_ref, near_ref):
    slabs = maps_ref.shape[0]
    me = lax.axis_index("gx")
    side = side_ref[me]
    fixed = side[0:QUAD]
    unit = side[QUAD : 2 * QUAD]
    forward = side[2 * QUAD : 3 * QUAD] > 0.5
    nothing = jnp.zeros_like(fixed)
    value = fixed
    near_ref[0] = nothing
    for i in range(slabs - 1, -1, -1):
        slab = maps_ref[i]
        entry_ref[i] = value
        if i < slabs - 1:
            near_ref[i + 1] = slab[2 * QUAD : 3 * QUAD] * value + slab[3 * QUAD : 4 * QUAD]
        value = slab[0:QUAD] * value + slab[QUAD : 2 * QUAD]
    near_ref[slabs] = slab[2 * QUAD : 3 * QUAD] * entry_ref[0] + slab[3 * QUAD : 4 * QUAD]
    leaving = value
    value = fixed
    answer = unit
    for i in range(slabs):
        slab = maps_ref[i]
        sent_ref[i, 0:QUAD] = jnp.where(forward, value, entry_ref[i])
        sent_ref[i, QUAD : 2 * QUAD] = jnp.where(forward, answer, leaving)
        value = slab[0:QUAD] * value + slab[QUAD : 2 * QUAD]
        answer = slab[0:QUAD] * answer
        upwind = near_ref[i] if i > 0 else nothing
        if i < slabs - 1:
            ahead = maps_ref[i + 1]
            step = ahead[2 * QUAD : 3 * QUAD]
            next_value = step * value + ahead[3 * QUAD : 4 * QUAD]
            next_answer = step * answer
        else:
            next_value = nothing
            next_answer = nothing
        sent_ref[i, 2 * QUAD : 3 * QUAD] = jnp.where(forward, next_value, upwind)
        sent_ref[i, 3 * QUAD : 4 * QUAD] = jnp.where(forward, next_answer, 0.0)


def whole_rows(back_ref, slot, tile, tiles, cells_y):
    return jnp.concatenate(
        [
            back_ref[quad * tiles + tile, slot * QUAD : (slot + 1) * QUAD]
            for quad in range(cells_y // QUAD)
        ],
        axis=0,
    )


def diffusivity(relax_ref, line_ref):
    cells_x, cells_y = relax_ref.shape
    line_ref[...] = jnp.zeros_like(line_ref)
    for x in range(cells_x):
        line_ref[0:1, x * cells_y : (x + 1) * cells_y] = relax_ref[x : x + 1, :]
    return 0.2 / (1.0 + line_ref[0:1, :])


def across_neighbours(m, cells_y):
    cells = m.shape[1]
    y = lax.broadcasted_iota(jnp.int32, m.shape, 1) % cells_y
    yp = jnp.where(y == cells_y - 1, pltpu.roll(m, cells_y - 1, 1), pltpu.roll(m, cells - 1, 1))
    ym = jnp.where(y == 0, pltpu.roll(m, cells - cells_y + 1, 1), pltpu.roll(m, 1, 1))
    return yp, ym


def moments_kernel(
    groups,
    slabs,
    reach_ref,
    run_ref,
    back_ref,
    velocity_ref,
    sign_ref,
    weight_ref,
    relax_ref,
    sent_ref,
    left_ref,
    psi_ref,
    line_ref,
):
    cells_x, cells_y, velocities = reach_ref.shape
    tiles = velocities // LANES
    cells = cells_x * cells_y
    half = left_ref.shape[0] // 2
    me = lax.axis_index("gx")
    from_left = jnp.where(me > 0, 1.0, 0.0)
    from_right = jnp.where(me < slabs - 1, 1.0, 0.0)

    def put(row, value, lanes):
        high = value.astype(jnp.bfloat16)
        low = (value - high.astype(jnp.float32)).astype(jnp.bfloat16)
        left_ref[row : row + cells_y, lanes] = high
        left_ref[half + row : half + row + cells_y, lanes] = low

    psi_ref[...] = jnp.zeros_like(psi_ref)
    for tile in range(tiles):
        lanes = slice(tile * LANES, (tile + 1) * LANES)
        magnitude, positive, cx, cy, cz, square = signed_velocity(velocity_ref, sign_ref, lanes)
        weight = weight_ref[0:1, lanes] / (velocities * groups)
        heat = 0.2 * (square - 2.5)
        moment_rows = [
            jnp.ones_like(cx),
            cx,
            cy,
            cz,
            2.0 / 3.0 * square - 1.0,
            2.0 * cx * cy,
            2.0 * cx * cz,
            2.0 * cy * cz,
            2.0 * (cx * cx - square / 3.0),
            2.0 * (cy * cy - square / 3.0),
            heat * cx,
            heat * cy,
            heat * cz,
            magnitude,
        ]
        for k, row in enumerate(moment_rows):
            value = weight * row
            high = value.astype(jnp.bfloat16).astype(jnp.float32)
            psi_ref[k : k + 1, lanes] = high
            psi_ref[16 + k : 17 + k, lanes] = value - high
        forward = jnp.broadcast_to(positive, (cells_y, LANES))
        entry = whole_rows(back_ref, 0, tile, tiles, cells_y)
        mixed = whole_rows(back_ref, 1, tile, tiles, cells_y)
        near = whole_rows(back_ref, 2, tile, tiles, cells_y)
        near_answer = whole_rows(back_ref, 3, tile, tiles, cells_y)
        answer = jnp.where(forward, mixed, 0.0)
        leaving = jnp.where(forward, 0.0, mixed)
        for x in range(cells_x):
            reach = reach_ref[x, :, lanes]
            put(x * cells_y, reach * entry + run_ref[x, :, lanes], lanes)
            put(cells + x * cells_y, reach * answer, lanes)
        row = 2 * cells
        put(row, jnp.where(forward, entry * from_left, near), lanes)
        put(row + cells_y, jnp.where(forward, near, entry * from_right), lanes)
        put(row + 2 * cells_y, answer * from_left, lanes)
        put(row + 3 * cells_y, near_answer, lanes)
        put(row + 4 * cells_y, leaving, lanes)
        put(row + 5 * cells_y, jnp.where(forward, 1.0, 0.0), lanes)
        put(row + 6 * cells_y, jnp.zeros_like(entry), lanes)
        put(row + 7 * cells_y, jnp.zeros_like(entry), lanes)

    product = lax.dot_general(
        left_ref[...],
        psi_ref[...].astype(jnp.bfloat16),
        (((1,), (1,)), ((), ())),
        preferred_element_type=jnp.float32,
    )
    upper = product[0:half]
    total = upper + pltpu.roll(upper, LANES - 16, 1) + product[half:]
    fixed = total[0:cells].T[0:16]
    answer = total[cells : 2 * cells].T[0:16]
    edges = total[2 * cells : 3 * cells].T[0:16]

    spread = diffusivity(relax_ref, line_ref)
    lane = lax.broadcasted_iota(jnp.int32, (16, cells), 1)

    def along(m, at_left, at_right):
        xm = jnp.where(lane < cells_y, at_left, pltpu.roll(m, cells_y, 1))
        xp = jnp.where(lane >= cells - cells_y, at_right, pltpu.roll(m, cells - cells_y, 1))
        dx = xp - xm
        flow = jnp.concatenate(
            [
                dx[1:2],
                dx[0:1] + dx[4:5] + dx[8:9],
                dx[5:6],
                dx[6:7],
                2.0 / 3.0 * (dx[1:2] + dx[10:11]),
            ],
            axis=0,
        )
        return (xp + xm - 4.0 * m)[0:5], flow

    def across(m):
        yp, ym = across_neighbours(m, cells_y)
        dy = yp - ym
        flow = jnp.concatenate(
            [
                dy[2:3],
                dy[5:6],
                dy[0:1] + dy[4:5] + dy[9:10],
                dy[7:8],
                2.0 / 3.0 * (dy[2:3] + dy[11:12]),
            ],
            axis=0,
        )
        return (yp + ym)[0:5], flow

    shifts = [0, cells - 2 * cells_y, cells - 2 * cells_y, cells - 4 * cells_y]
    placed = [edges if s == 0 else pltpu.roll(edges, s, 1) for s in shifts]
    laplace, flow = along(fixed, placed[0], placed[1])
    laplace_across, flow_across = across(fixed)
    change = spread * (laplace + laplace_across) - 0.25 * (flow + flow_across)
    laplace, flow = along(answer, placed[2], placed[3])
    change_answer = spread * laplace - 0.25 * flow
    message = jnp.concatenate(
        [
            fixed[0:5],
            change,
            answer[0:5],
            answer[5:6],
            answer[7:8],
            answer[9:10],
            answer[11:12],
            change_answer,
            edges[13:14],
            jnp.zeros((SENT_ROWS - 25, cells), jnp.float32),
        ],
        axis=0,
    )
    for group in range(groups):
        sent_ref[group] = message


def finish_kernel(
    parts_ref,
    reach_ref,
    run_ref,
    back_ref,
    velocity_ref,
    sign_ref,
    relax_ref,
    state_ref,
    macro_ref,
    spread_ref,
    line_ref,
):
    cells_x, cells_y, velocities = reach_ref.shape
    groups = parts_ref.shape[0]
    tiles = velocities // LANES
    cells = cells_x * cells_y
    total = parts_ref[0]
    for group in range(1, groups):
        total = total + parts_ref[group]
    lane = lax.broadcasted_iota(jnp.int32, (1, cells), 1)
    sums = total[24:25]
    here = jnp.logical_and(lane >= 4 * cells_y, lane < 5 * cells_y)
    incoming = jnp.where(here, pltpu.roll(sums, cells - cells_y, 1), 1.0)
    rho = jnp.where(here, sums, 0.0) / incoming
    width = cells_y
    while width < cells:
        rho = rho + pltpu.roll(rho, width, 1)
        width *= 2
    answer = rho * total[8:24]
    yp, ym = across_neighbours(answer, cells_y)
    dy = yp - ym
    flow = jnp.concatenate(
        [
            dy[4:5],
            dy[7:8],
            dy[2:3] + dy[6:7] + dy[9:10],
            dy[8:9],
            2.0 / 3.0 * (dy[4:5] + dy[10:11]),
        ],
        axis=0,
    )
    spread = diffusivity(relax_ref, line_ref)
    change = total[5:10] + rho * total[19:24] + spread * (yp + ym)[2:7] - 0.25 * flow
    updated = total[0:5] + answer[2:7] + change
    for x in range(cells_x):
        macro_ref[:, x, :] = updated[:, x * cells_y : (x + 1) * cells_y]
    columns = jnp.concatenate([change, rho, jnp.zeros((2, cells), jnp.float32)], axis=0).T
    for x in range(cells_x):
        for k in range(5):
            spread_ref[k * cells_x + x] = jnp.broadcast_to(
                columns[x * cells_y : (x + 1) * cells_y, k : k + 1], (cells_y, LANES)
            )
    density = jnp.broadcast_to(columns[0:cells_y, 5:6], (cells_y, LANES))
    for tile in range(tiles):
        lanes = slice(tile * LANES, (tile + 1) * LANES)
        _, positive, cx, cy, cz, square = signed_velocity(velocity_ref, sign_ref, lanes)
        basis = [2.0 * cx, 2.0 * cy, 2.0 * cz, square - 1.5]
        forward = jnp.broadcast_to(positive, (cells_y, LANES))
        entry = whole_rows(back_ref, 0, tile, tiles, cells_y)
        mixed = whole_rows(back_ref, 1, tile, tiles, cells_y)
        entry = entry + jnp.where(forward, density * mixed, 0.0)
        for x in range(cells_x):
            value = reach_ref[x, :, lanes] * entry + run_ref[x, :, lanes] + spread_ref[x]
            for k in range(1, 5):
                value = value + spread_ref[k * cells_x + x] * basis[k - 1]
            state_ref[x, :, lanes] = value


def local(state, macro, relax_rate, velocity, vel_sign, quad_weight, freestream, wall_flag):
    cells_x, cells_y, velocities = state.shape
    fields = macro.shape[0]
    slabs = lax.axis_size("gx")
    groups = lax.axis_size("vert")
    cells = cells_x * cells_y
    tiles = velocities // LANES
    assert slabs == tiles * (cells_y // QUAD) and cells == LANES
    f32 = jnp.float32
    sign = vel_sign.reshape(1, velocities)
    weight = quad_weight.reshape(1, velocities)
    wall = wall_flag.reshape(1, cells_y)
    shape = jax.ShapeDtypeStruct

    def call(body, outs, scratch, *args):
        return pl.pallas_call(
            body, out_shape=outs, scratch_shapes=scratch, interpret=INTERPRET
        )(*args)

    reach, run, sent, side = call(
        lambda *refs: maps_kernel(float(cells_x * slabs), *refs),
        (
            shape(state.shape, f32),
            shape(state.shape, f32),
            shape((slabs, 4 * QUAD, LANES), f32),
            shape((slabs, 4 * QUAD, LANES), f32),
        ),
        [
            pltpu.VMEM((fields * cells_x + 2 * cells_x, LANES), f32),
            pltpu.VMEM((fields * cells_x + cells_x + 1, cells_y, LANES), f32),
        ],
        state,
        macro,
        relax_rate,
        velocity,
        sign,
        freestream,
        wall,
    )
    maps = lax.all_to_all(sent, "gx", 0, 0)
    entries = call(
        scan_kernel,
        shape((slabs, 4 * QUAD, LANES), f32),
        [
            pltpu.VMEM((slabs, QUAD, LANES), f32),
            pltpu.VMEM((slabs + 1, QUAD, LANES), f32),
        ],
        maps,
        side,
    )
    back = lax.all_to_all(entries, "gx", 0, 0)
    partial_sums = call(
        lambda *refs: moments_kernel(groups, slabs, *refs),
        shape((groups, SENT_ROWS, cells), f32),
        [
            pltpu.VMEM((6 * cells, velocities), jnp.bfloat16),
            pltpu.VMEM((LANES, velocities), f32),
            pltpu.VMEM((8, cells), f32),
        ],
        reach,
        run,
        back,
        velocity,
        sign,
        weight,
        relax_rate,
    )
    parts = lax.all_to_all(partial_sums, "vert", 0, 0)
    new_state, new_macro = call(
        finish_kernel,
        (shape(state.shape, f32), shape(macro.shape, f32)),
        [pltpu.VMEM((5 * cells_x, cells_y, LANES), f32), pltpu.VMEM((8, cells), f32)],
        parts,
        reach,
        run,
        back,
        velocity,
        sign,
        relax_rate,
    )
    return new_state, new_macro


def solution(mesh):
    return jax.shard_map(
        local,
        mesh=mesh,
        in_specs=(
            P("gx", None, "vert"),
            P(None, "gx", None),
            P("gx", None),
            P(None, "vert"),
            P("vert"),
            P("vert"),
            P(None, "vert"),
            P(),
        ),
        out_specs=(P("gx", None, "vert"), P(None, "gx", None)),
        check_vma=False,
    )
```

time: 476 us -> 75.1 us (0.16)
  the two profiles are of different devices: /device:TPU:7 before, /device:TPU:32 now
where the time goes in v1:
time: 75.1 us; the launch traced here: 74.6 us
  blocking collectives  63.4 us (84%)
  Pallas kernels  10.6 us (14%)
    all_to_all x1, blocking collectives, local(): parts = lax.all_to_all(partial_sums, 'vert', 0, 0)  33.9 us
    all_to_all x1, blocking collectives, local(): maps = lax.all_to_all(sent, 'gx', 0, 0)  16.2 us
    all_to_all x1, blocking collectives, local(): back = lax.all_to_all(entries, 'gx', 0, 0)  13.3 us
    pallas_call x4, Pallas kernels, call(): pl.pallas_call(body, out_shape=outs, scratch_shapes=scratch, interpret=IN...  10.6 us

profile of v1, /device:TPU:32, one launch (start us, length us, event | category | flops | bytes accessed | tf_op | source)
XLA Modules:
  0.0 74.6 jit_solution(15858563249340771885)
XLA Ops:
  0.6 2.9 %shard_map.95 = (f32[8,16,1024]{2,1,0:T(8,128)}, f32[8,16,1024]{2,1,0:T(8,128)}, f32[32,16,128]{2,1,0:T(8,128)}, f32[32,16,128]{2,1,0:T(8,128)}) custom-call(f32[8,16,1024]{2,1,0:T(8,128)} %refs_0_.1, f32[5,8,16]{2,1,0:T(8,128)} %refs_1_.1, f32[8,16]{1,0:T(8,128)} %relax_ref.1, f32[3,1024]{1,0:T(4,128)} %velocity_ref.1, s32[1,1024]{1,0:T(1,128)} %bitcast.3, ...), custom_call_target="tpu_custom_call" | custom-call | tf_op jit(solution)/shard_map/pallas_call | solution.py:397
  3.5 16.2 %all_to_all.15.maps_ref = f32[32,16,128]{2,1,0:T(8,128)} all-to-all(f32[32,16,128]{2,1,0:T(8,128)} %get-tuple-element.8), channel_id=1, replica_groups=mesh['gx'=32,'vert'=16] {'gx'}, dimensions={0} | all-to-all | bytes 524288 | tf_op jit(solution)/shard_map/all_to_all | solution.py:421
  19.7 1.8 %shard_map.96 = f32[32,16,128]{2,1,0:T(8,128)} custom-call(f32[32,16,128]{2,1,0:T(8,128)} %all_to_all.15.maps_ref, f32[32,16,128]{2,1,0:T(8,128)} %get-tuple-element.9.side_ref), custom_call_target="tpu_custom_call" | custom-call | tf_op jit(solution)/shard_map/pallas_call | solution.py:397
  21.5 13.3 %all_to_all.16.refs_2_.back_ref = f32[32,16,128]{2,1,0:T(8,128)} all-to-all(f32[32,16,128]{2,1,0:T(8,128)} %shard_map.96), channel_id=1, replica_groups=mesh['gx'=32,'vert'=16] {'gx'}, dimensions={0} | all-to-all | bytes 524288 | tf_op jit(solution)/shard_map/all_to_all | solution.py:432
  34.9 3.0 %shard_map.97 = f32[16,32,128]{2,1,0:T(8,128)} custom-call(f32[8,16,1024]{2,1,0:T(8,128)} %get-tuple-element.6.refs_0_.reach_ref, f32[8,16,1024]{2,1,0:T(8,128)} %get-tuple-element.7.refs_1_.run_ref, f32[32,16,128]{2,1,0:T(8,128)} %all_to_all.16.refs_2_.back_ref, f32[3,1024]{1,0:T(4,128)} %velocity_ref.1, s32[1,1024]{1,0:T(1,128)} %bitcast.4, ...), custom_call_target="tpu_custom_call" | custom-call | tf_op jit(solution)/shard_map/pallas_call | solution.py:397
  37.8 33.9 %all_to_all.17.parts_ref = f32[16,32,128]{2,1,0:T(8,128)} all-to-all(f32[16,32,128]{2,1,0:T(8,128)} %shard_map.97), channel_id=1, replica_groups=mesh['gx'=32,'vert'=16] {'vert'}, dimensions={0} | all-to-all | bytes 524288 | tf_op jit(solution)/shard_map/all_to_all | solution.py:449
  71.7 3.0 %shard_map.98 = (f32[8,16,1024]{2,1,0:T(8,128)}, f32[5,8,16]{2,1,0:T(8,128)}) custom-call(f32[16,32,128]{2,1,0:T(8,128)} %all_to_all.17.parts_ref, f32[8,16,1024]{2,1,0:T(8,128)} %get-tuple-element.6.refs_0_.reach_ref, f32[8,16,1024]{2,1,0:T(8,128)} %get-tuple-element.7.refs_1_.run_ref, f32[32,16,128]{2,1,0:T(8,128)} %all_to_all.16.refs_2_.back_ref, ...), custom_call_target="tpu_custom_call" | custom-call | tf_op jit(solution)/shard_map/pallas_call | solution.py:397

commit v2 on v1

--- a/solution.py
+++ b/solution.py
@@ -392,6 +392,10 @@
     weight = quad_weight.reshape(1, velocities)
     wall = wall_flag.reshape(1, cells_y)
     shape = jax.ShapeDtypeStruct
+    near = shape if INTERPRET else pltpu.VMEM
+
+    def held(x):
+        return x if INTERPRET else pltpu.with_memory_space_constraint(x, pltpu.VMEM)
 
     def call(body, outs, scratch, *args):
         return pl.pallas_call(
@@ -401,10 +405,10 @@
     reach, run, sent, side = call(
         lambda *refs: maps_kernel(float(cells_x * slabs), *refs),
         (
-            shape(state.shape, f32),
-            shape(state.shape, f32),
-            shape((slabs, 4 * QUAD, LANES), f32),
-            shape((slabs, 4 * QUAD, LANES), f32),
+            near(state.shape, f32),
+            near(state.shape, f32),
+            near((slabs, 4 * QUAD, LANES), f32),
+            near((slabs, 4 * QUAD, LANES), f32),
         ),
         [
             pltpu.VMEM((fields * cells_x + 2 * cells_x, LANES), f32),
@@ -418,10 +422,11 @@
         freestream,
         wall,
     )
-    maps = lax.all_to_all(sent, "gx", 0, 0)
+    reach, run, side = (held(value) for value in (reach, run, side))
+    maps = held(lax.all_to_all(sent, "gx", 0, 0))
     entries = call(
         scan_kernel,
-        shape((slabs, 4 * QUAD, LANES), f32),
+        near((slabs, 4 * QUAD, LANES), f32),
         [
             pltpu.VMEM((slabs, QUAD, LANES), f32),
             pltpu.VMEM((slabs + 1, QUAD, LANES), f32),
@@ -429,10 +434,10 @@
         maps,
         side,
     )
-    back = lax.all_to_all(entries, "gx", 0, 0)
+    back = held(lax.all_to_all(entries, "gx", 0, 0))
     partial_sums = call(
         lambda *refs: moments_kernel(groups, slabs, *refs),
-        shape((groups, SENT_ROWS, cells), f32),
+        near((groups, SENT_ROWS, cells), f32),
         [
             pltpu.VMEM((6 * cells, velocities), jnp.bfloat16),
             pltpu.VMEM((LANES, velocities), f32),
@@ -446,7 +451,7 @@
         weight,
         relax_rate,
     )
-    parts = lax.all_to_all(partial_sums, "vert", 0, 0)
+    parts = held(lax.all_to_all(partial_sums, "vert", 0, 0))
     new_state, new_macro = call(
         finish_kernel,
         (shape(state.shape, f32), shape(macro.shape, f32)),

time: 75.1 us -> 68.7 us (0.915)
  Pallas kernels: 10.6 us -> 5.82 us
  blocking collectives: 63.4 us -> 61.9 us
    pallas_call x4, Pallas kernels: 10.6 us -> 5.82 us  [call(): pl.pallas_call(body, out_shape=outs, scratch_shapes=scratch, interpret=IN...]
    all_to_all x3, blocking collectives: 63.4 us -> 61.9 us  [the longest x1 33.6 us: local(): parts = held(lax.all_to_all(partial_sums, 'vert', 0, 0))]
where the time goes in v2:
time: 68.7 us; the launch traced here: 68.4 us
  blocking collectives  61.9 us (90%)
  Pallas kernels  5.82 us (8%)
    all_to_all x1, blocking collectives, local(): parts = held(lax.all_to_all(partial_sums, 'vert', 0, 0))  33.6 us
    all_to_all x1, blocking collectives, local(): maps = held(lax.all_to_all(sent, 'gx', 0, 0))  15.9 us
    all_to_all x1, blocking collectives, local(): back = held(lax.all_to_all(entries, 'gx', 0, 0))  12.4 us
    pallas_call x4, Pallas kernels, call(): pl.pallas_call(body, out_shape=outs, scratch_shapes=scratch, interpret=IN...  5.82 us

profile of v2, /device:TPU:32, one launch (start us, length us, event | category | flops | bytes accessed | tf_op | source)
XLA Modules:
  0.0 68.4 jit_solution(14478753340873198811)
XLA Ops:
  0.6 1.7 %shard_map.95 = (f32[8,16,1024]{2,1,0:T(8,128)S(1)}, f32[8,16,1024]{2,1,0:T(8,128)S(1)}, f32[32,16,128]{2,1,0:T(8,128)S(1)}, f32[32,16,128]{2,1,0:T(8,128)S(1)}) custom-call(f32[8,16,1024]{2,1,0:T(8,128)} %refs_0_.1, f32[5,8,16]{2,1,0:T(8,128)} %refs_1_.1, f32[8,16]{1,0:T(8,128)} %relax_ref.1, f32[3,1024]{1,0:T(4,128)} %velocity_ref.1, s32[1,1024]{1,0:T(1,128)} %bitcast.3, ...), custom_call_target="tpu_custom_call" | custom-call | tf_op jit(solution)/shard_map/pallas_call | solution.py:401
  2.4 15.9 %all_to_all.15.maps_ref = f32[32,16,128]{2,1,0:T(8,128)S(1)} all-to-all(f32[32,16,128]{2,1,0:T(8,128)S(1)} %get-tuple-element.8), channel_id=1, replica_groups=mesh['gx'=32,'vert'=16] {'gx'}, dimensions={0} | all-to-all | bytes 524288 | tf_op jit(solution)/shard_map/all_to_all | solution.py:426
  18.3 0.1 shard_map.96
  18.4 12.4 %all_to_all.16.refs_2_.back_ref = f32[32,16,128]{2,1,0:T(8,128)S(1)} all-to-all(f32[32,16,128]{2,1,0:T(8,128)S(1)} %shard_map.96), channel_id=1, replica_groups=mesh['gx'=32,'vert'=16] {'gx'}, dimensions={0} | all-to-all | bytes 524288 | tf_op jit(solution)/shard_map/all_to_all | solution.py:437
  30.8 1.7 %shard_map.97 = f32[16,32,128]{2,1,0:T(8,128)S(1)} custom-call(f32[8,16,1024]{2,1,0:T(8,128)S(1)} %get-tuple-element.6.refs_0_.reach_ref, f32[8,16,1024]{2,1,0:T(8,128)S(1)} %get-tuple-element.7.refs_1_.run_ref, f32[32,16,128]{2,1,0:T(8,128)S(1)} %all_to_all.16.refs_2_.back_ref, f32[3,1024]{1,0:T(4,128)} %velocity_ref.1, s32[1,1024]{1,0:T(1,128)} %bitcast.4, ...), custom_call_target="tpu_custom_call" | custom-call | tf_op jit(solution)/shard_map/pallas_call | solution.py:401
  32.5 33.6 %all_to_all.17.parts_ref = f32[16,32,128]{2,1,0:T(8,128)S(1)} all-to-all(f32[16,32,128]{2,1,0:T(8,128)S(1)} %shard_map.97), channel_id=1, replica_groups=mesh['gx'=32,'vert'=16] {'vert'}, dimensions={0} | all-to-all | bytes 524288 | tf_op jit(solution)/shard_map/all_to_all | solution.py:454
  66.0 2.3 %shard_map.98 = (f32[8,16,1024]{2,1,0:T(8,128)}, f32[5,8,16]{2,1,0:T(8,128)}) custom-call(f32[16,32,128]{2,1,0:T(8,128)S(1)} %all_to_all.17.parts_ref, f32[8,16,1024]{2,1,0:T(8,128)S(1)} %get-tuple-element.6.refs_0_.reach_ref, f32[8,16,1024]{2,1,0:T(8,128)S(1)} %get-tuple-element.7.refs_1_.run_ref, f32[32,16,128]{2,1,0:T(8,128)S(1)} %all_to_all.16.refs_2_.back_ref, ...), custom_call_target="tpu_custom_call" | custom-call | tf_op jit(solution)/shard_map/pallas_call | solution.py:401

commit v3 on v2

--- a/solution.py
+++ b/solution.py
@@ -7,39 +7,74 @@
 
 LANES = 128
 QUAD = 4
-SENT_ROWS = 32
+SENT_PARTS = 7
 INTERPRET = False
-
-
-def signed_velocity(velocity_ref, sign_ref, lanes):
-    magnitude = velocity_ref[0:1, lanes]
-    positive = sign_ref[0:1, lanes] == 1
-    along_x = jnp.where(positive, magnitude, -magnitude)
-    along_y = velocity_ref[1:2, lanes]
-    along_z = velocity_ref[2:3, lanes]
-    square = along_x * along_x + along_y * along_y + along_z * along_z
-    return magnitude, positive, along_x, along_y, along_z, square
 
 
 def maps_kernel(
     total_cells,
+    groups,
+    state_hbm,
+    macro_hbm,
+    relax_hbm,
+    velocity_hbm,
+    sign_hbm,
+    weight_hbm,
+    free_hbm,
+    wall_hbm,
+    reach_ref,
+    run_ref,
+    sent_ref,
+    side_ref,
+    psi_ref,
+    table_ref,
+    line_ref,
     state_ref,
     macro_ref,
     relax_ref,
     velocity_ref,
     sign_ref,
+    weight_ref,
     free_ref,
     wall_ref,
-    reach_ref,
-    run_ref,
-    sent_ref,
-    side_ref,
     pad_ref,
     spread_ref,
+    sems,
 ):
     fields, cells_x, cells_y = macro_ref.shape
-    tiles = state_ref.shape[2] // LANES
+    velocities = state_ref.shape[2]
+    tiles = velocities // LANES
+    halves = cells_y // 8
+    small = [
+        pltpu.make_async_copy(source, target, sems.at[halves + n])
+        for n, (source, target) in enumerate(
+            (
+                (velocity_hbm, velocity_ref),
+                (sign_hbm, sign_ref),
+                (weight_hbm, weight_ref),
+                (macro_hbm, macro_ref),
+                (relax_hbm, relax_ref),
+                (wall_hbm, wall_ref),
+                (free_hbm, free_ref),
+            )
+        )
+    ]
+    large = [
+        pltpu.make_async_copy(
+            state_hbm.at[:, pl.ds(half * 8, 8), :],
+            state_ref.at[:, pl.ds(half * 8, 8), :],
+            sems.at[half],
+        )
+        for half in range(halves)
+    ]
+    for copy in small + large:
+        copy.start()
     pad_ref[...] = jnp.zeros_like(pad_ref)
+    psi_ref[...] = jnp.zeros_like(psi_ref)
+    table_ref[...] = jnp.zeros_like(table_ref)
+    line_ref[...] = jnp.zeros_like(line_ref)
+    for copy in small:
+        copy.wait()
     for k in range(fields):
         pad_ref[k * cells_x : (k + 1) * cells_x, 0:cells_y] = macro_ref[k]
     base_row = fields * cells_x
@@ -49,17 +84,62 @@
     columns = pad_ref[...].T
     for c in range(wall_row + 1):
         spread_ref[c] = jnp.broadcast_to(columns[0:cells_y, c : c + 1], (cells_y, LANES))
-    for tile in range(tiles):
-        lanes = slice(tile * LANES, (tile + 1) * LANES)
-        magnitude, positive, along_x, along_y, along_z, square = signed_velocity(
-            velocity_ref, sign_ref, lanes
-        )
-        courant = total_cells * magnitude
-        base = 1.0 + courant
-        basis = [2.0 * along_x, 2.0 * along_y, 2.0 * along_z, square - 1.5]
-        for half in range(cells_y // 8):
-            rows = slice(half * 8, half * 8 + 8)
-            forward = jnp.broadcast_to(positive, (8, LANES))
+    for x in range(cells_x):
+        line_ref[0:1, x * cells_y : (x + 1) * cells_y] = relax_ref[x : x + 1, :]
+    line_ref[0:1, :] = 0.2 / (1.0 + line_ref[0:1, :])
+
+    magnitude = velocity_ref[0:1, :]
+    positive = sign_ref[...] == 1
+    cx = jnp.where(positive, magnitude, -magnitude)
+    cy = velocity_ref[1:2, :]
+    cz = velocity_ref[2:3, :]
+    square = cx * cx + cy * cy + cz * cz
+    for k, row in enumerate(
+        (
+            2.0 * cx,
+            2.0 * cy,
+            2.0 * cz,
+            square - 1.5,
+            jnp.where(positive, 1.0, 0.0),
+            total_cells * magnitude,
+        )
+    ):
+        table_ref[k : k + 1, :] = row
+    weight = weight_ref[...] / (velocities * groups)
+    heat = 0.2 * (square - 2.5)
+    for k, row in enumerate(
+        (
+            jnp.ones_like(cx),
+            cx,
+            cy,
+            cz,
+            2.0 / 3.0 * square - 1.0,
+            2.0 * cx * cy,
+            2.0 * cx * cz,
+            2.0 * cy * cz,
+            2.0 * (cx * cx - square / 3.0),
+            2.0 * (cy * cy - square / 3.0),
+            heat * cx,
+            heat * cy,
+            heat * cz,
+            magnitude,
+        )
+    ):
+        value = weight * row
+        high = value.astype(jnp.bfloat16).astype(jnp.float32)
+        psi_ref[k : k + 1, :] = high
+        psi_ref[16 + k : 17 + k, :] = value - high
+
+    last = cells_x - 1
+    for half in range(halves):
+        large[half].wait()
+        rows = slice(half * 8, half * 8 + 8)
+        for tile in range(tiles):
+            lanes = slice(tile * LANES, (tile + 1) * LANES)
+            forward = jnp.broadcast_to(table_ref[4:5, lanes], (8, LANES)) > 0.5
+            courant = jnp.broadcast_to(table_ref[5:6, lanes], (8, LANES))
+            base = 1.0 + courant
+            basis = [jnp.broadcast_to(table_ref[k : k + 1, lanes], (8, LANES)) for k in range(4)]
             decay = []
             driven = []
             for x in range(cells_x):
@@ -70,7 +150,6 @@
                 inverse = 1.0 / (base + relax)
                 decay.append(courant * inverse)
                 driven.append((state_ref[x, rows, lanes] + relax * equil) * inverse)
-            last = cells_x - 1
             steps = [jnp.where(forward, decay[t], decay[last - t]) for t in range(cells_x)]
             gains = [jnp.where(forward, driven[t], driven[last - t]) for t in range(cells_x)]
             products = [steps[0]]
@@ -82,9 +161,8 @@
                 reach_ref[x, rows, lanes] = jnp.where(forward, products[x], products[last - x])
                 run_ref[x, rows, lanes] = jnp.where(forward, runs[x], runs[last - x])
             wall = spread_ref[wall_row, rows] > 0.5
-            free = free_ref[rows, lanes]
             diffuse = jnp.logical_and(forward, wall)
-            fixed = jnp.where(diffuse, 0.0, free)
+            fixed = jnp.where(diffuse, 0.0, free_ref[rows, lanes])
             unit = jnp.where(diffuse, 1.0, 0.0)
             direction = jnp.where(forward, 1.0, 0.0)
             for part in range(8 // QUAD):
@@ -145,14 +223,6 @@
     )
 
 
-def diffusivity(relax_ref, line_ref):
-    cells_x, cells_y = relax_ref.shape
-    line_ref[...] = jnp.zeros_like(line_ref)
-    for x in range(cells_x):
-        line_ref[0:1, x * cells_y : (x + 1) * cells_y] = relax_ref[x : x + 1, :]
-    return 0.2 / (1.0 + line_ref[0:1, :])
-
-
 def across_neighbours(m, cells_y):
     cells = m.shape[1]
     y = lax.broadcasted_iota(jnp.int32, m.shape, 1) % cells_y
@@ -162,19 +232,7 @@
 
 
 def moments_kernel(
-    groups,
-    slabs,
-    reach_ref,
-    run_ref,
-    back_ref,
-    velocity_ref,
-    sign_ref,
-    weight_ref,
-    relax_ref,
-    sent_ref,
-    left_ref,
-    psi_ref,
-    line_ref,
+    groups, slabs, reach_ref, run_ref, back_ref, psi_ref, table_ref, line_ref, sent_ref, left_ref
 ):
     cells_x, cells_y, velocities = reach_ref.shape
     tiles = velocities // LANES
@@ -190,33 +248,9 @@
         left_ref[row : row + cells_y, lanes] = high
         left_ref[half + row : half + row + cells_y, lanes] = low
 
-    psi_ref[...] = jnp.zeros_like(psi_ref)
     for tile in range(tiles):
         lanes = slice(tile * LANES, (tile + 1) * LANES)
-        magnitude, positive, cx, cy, cz, square = signed_velocity(velocity_ref, sign_ref, lanes)
-        weight = weight_ref[0:1, lanes] / (velocities * groups)
-        heat = 0.2 * (square - 2.5)
-        moment_rows = [
-            jnp.ones_like(cx),
-            cx,
-            cy,
-            cz,
-            2.0 / 3.0 * square - 1.0,
-            2.0 * cx * cy,
-            2.0 * cx * cz,
-            2.0 * cy * cz,
-            2.0 * (cx * cx - square / 3.0),
-            2.0 * (cy * cy - square / 3.0),
-            heat * cx,
-            heat * cy,
-            heat * cz,
-            magnitude,
-        ]
-        for k, row in enumerate(moment_rows):
-            value = weight * row
-            high = value.astype(jnp.bfloat16).astype(jnp.float32)
-            psi_ref[k : k + 1, lanes] = high
-            psi_ref[16 + k : 17 + k, lanes] = value - high
+        positive = table_ref[4:5, lanes] > 0.5
         forward = jnp.broadcast_to(positive, (cells_y, LANES))
         entry = whole_rows(back_ref, 0, tile, tiles, cells_y)
         mixed = whole_rows(back_ref, 1, tile, tiles, cells_y)
@@ -245,12 +279,12 @@
         preferred_element_type=jnp.float32,
     )
     upper = product[0:half]
-    total = upper + pltpu.roll(upper, LANES - 16, 1) + product[half:]
-    fixed = total[0:cells].T[0:16]
-    answer = total[cells : 2 * cells].T[0:16]
-    edges = total[2 * cells : 3 * cells].T[0:16]
-
-    spread = diffusivity(relax_ref, line_ref)
+    total = upper[:, 0:16] + upper[:, 16:32] + product[half:, 0:16]
+    fixed = total[0:cells].T
+    answer = total[cells : 2 * cells].T
+    edges = total[2 * cells : 3 * cells].T
+
+    spread = line_ref[0:1, :]
     lane = lax.broadcasted_iota(jnp.int32, (16, cells), 1)
 
     def along(m, at_left, at_right):
@@ -291,23 +325,23 @@
     change = spread * (laplace + laplace_across) - 0.25 * (flow + flow_across)
     laplace, flow = along(answer, placed[2], placed[3])
     change_answer = spread * laplace - 0.25 * flow
-    message = jnp.concatenate(
-        [
-            fixed[0:5],
-            change,
-            answer[0:5],
-            answer[5:6],
-            answer[7:8],
-            answer[9:10],
-            answer[11:12],
-            change_answer,
-            edges[13:14],
-            jnp.zeros((SENT_ROWS - 25, cells), jnp.float32),
-        ],
-        axis=0,
-    )
-    for group in range(groups):
-        sent_ref[group] = message
+    message = [
+        fixed[0:5],
+        change,
+        answer[0:5],
+        answer[5:6],
+        answer[7:8],
+        answer[9:10],
+        answer[11:12],
+        change_answer,
+        edges[13:14],
+    ]
+    spare = QUAD * (sent_ref.shape[2] // cells) - 25
+    message = jnp.concatenate(message + [jnp.zeros((spare, cells), jnp.float32)], axis=0)
+    for part in range(sent_ref.shape[2] // cells):
+        piece = message[part * QUAD : (part + 1) * QUAD]
+        for group in range(groups):
+            sent_ref[group, :, part * cells : (part + 1) * cells] = piece
 
 
 def finish_kernel(
@@ -315,21 +349,27 @@
     reach_ref,
     run_ref,
     back_ref,
-    velocity_ref,
-    sign_ref,
-    relax_ref,
+    table_ref,
+    line_ref,
+    state_hbm,
+    macro_hbm,
     state_ref,
     macro_ref,
     spread_ref,
-    line_ref,
+    entry_ref,
+    sems,
 ):
     cells_x, cells_y, velocities = reach_ref.shape
     groups = parts_ref.shape[0]
     tiles = velocities // LANES
     cells = cells_x * cells_y
-    total = parts_ref[0]
-    for group in range(1, groups):
-        total = total + parts_ref[group]
+    sums = [parts_ref[group] for group in range(groups)]
+    while len(sums) > 1:
+        sums = [sums[n] + sums[n + 1] for n in range(0, len(sums), 2)]
+    total = jnp.concatenate(
+        [sums[0][:, n * cells : (n + 1) * cells] for n in range(parts_ref.shape[2] // cells)],
+        axis=0,
+    )
     lane = lax.broadcasted_iota(jnp.int32, (1, cells), 1)
     sums = total[24:25]
     here = jnp.logical_and(lane >= 4 * cells_y, lane < 5 * cells_y)
@@ -352,11 +392,13 @@
         ],
         axis=0,
     )
-    spread = diffusivity(relax_ref, line_ref)
+    spread = line_ref[0:1, :]
     change = total[5:10] + rho * total[19:24] + spread * (yp + ym)[2:7] - 0.25 * flow
     updated = total[0:5] + answer[2:7] + change
     for x in range(cells_x):
         macro_ref[:, x, :] = updated[:, x * cells_y : (x + 1) * cells_y]
+    macro_copy = pltpu.make_async_copy(macro_ref, macro_hbm, sems.at[cells_x])
+    macro_copy.start()
     columns = jnp.concatenate([change, rho, jnp.zeros((2, cells), jnp.float32)], axis=0).T
     for x in range(cells_x):
         for k in range(5):
@@ -366,17 +408,29 @@
     density = jnp.broadcast_to(columns[0:cells_y, 5:6], (cells_y, LANES))
     for tile in range(tiles):
         lanes = slice(tile * LANES, (tile + 1) * LANES)
-        _, positive, cx, cy, cz, square = signed_velocity(velocity_ref, sign_ref, lanes)
-        basis = [2.0 * cx, 2.0 * cy, 2.0 * cz, square - 1.5]
-        forward = jnp.broadcast_to(positive, (cells_y, LANES))
+        forward = jnp.broadcast_to(table_ref[4:5, lanes], (cells_y, LANES)) > 0.5
         entry = whole_rows(back_ref, 0, tile, tiles, cells_y)
         mixed = whole_rows(back_ref, 1, tile, tiles, cells_y)
-        entry = entry + jnp.where(forward, density * mixed, 0.0)
-        for x in range(cells_x):
-            value = reach_ref[x, :, lanes] * entry + run_ref[x, :, lanes] + spread_ref[x]
-            for k in range(1, 5):
-                value = value + spread_ref[k * cells_x + x] * basis[k - 1]
-            state_ref[x, :, lanes] = value
+        entry_ref[:, lanes] = entry + jnp.where(forward, density * mixed, 0.0)
+    copies = []
+    span = 2
+    for first in range(0, cells_x, span):
+        for tile in range(tiles):
+            lanes = slice(tile * LANES, (tile + 1) * LANES)
+            basis = [table_ref[k : k + 1, lanes] for k in range(4)]
+            entry = entry_ref[:, lanes]
+            for x in range(first, first + span):
+                value = reach_ref[x, :, lanes] * entry + run_ref[x, :, lanes] + spread_ref[x]
+                for k in range(1, 5):
+                    value = value + spread_ref[k * cells_x + x] * basis[k - 1]
+                state_ref[x, :, lanes] = value
+        copy = pltpu.make_async_copy(
+            state_ref.at[pl.ds(first, span)], state_hbm.at[pl.ds(first, span)], sems.at[first]
+        )
+        copy.start()
+        copies.append(copy)
+    for copy in copies + [macro_copy]:
+        copy.wait()
 
 
 def local(state, macro, relax_rate, velocity, vel_sign, quad_weight, freestream, wall_flag):
@@ -397,36 +451,39 @@
     def held(x):
         return x if INTERPRET else pltpu.with_memory_space_constraint(x, pltpu.VMEM)
 
-    def call(body, outs, scratch, *args):
+    def call(body, outs, scratch, *args, **kwargs):
         return pl.pallas_call(
-            body, out_shape=outs, scratch_shapes=scratch, interpret=INTERPRET
+            body, out_shape=outs, scratch_shapes=scratch, interpret=INTERPRET, **kwargs
         )(*args)
 
-    reach, run, sent, side = call(
-        lambda *refs: maps_kernel(float(cells_x * slabs), *refs),
+    anywhere = pl.BlockSpec(memory_space=pl.ANY)
+    sources = (state, macro, relax_rate, velocity, sign, weight, freestream, wall)
+    exchanged = near((slabs, 4 * QUAD, LANES), f32)
+    reach, run, sent, side, psi, table, line = call(
+        lambda *refs: maps_kernel(float(cells_x * slabs), groups, *refs),
         (
             near(state.shape, f32),
             near(state.shape, f32),
-            near((slabs, 4 * QUAD, LANES), f32),
-            near((slabs, 4 * QUAD, LANES), f32),
+            exchanged,
+            exchanged,
+            near((32, velocities), f32),
+            near((8, velocities), f32),
+            near((8, cells), f32),
         ),
-        [
+        [pltpu.VMEM(value.shape, value.dtype) for value in sources]
+        + [
             pltpu.VMEM((fields * cells_x + 2 * cells_x, LANES), f32),
             pltpu.VMEM((fields * cells_x + cells_x + 1, cells_y, LANES), f32),
+            pltpu.SemaphoreType.DMA((cells_y // 8 + 7,)),
         ],
-        state,
-        macro,
-        relax_rate,
-        velocity,
-        sign,
-        freestream,
-        wall,
-    )
-    reach, run, side = (held(value) for value in (reach, run, side))
+        *sources,
+        in_specs=[anywhere] * len(sources),
+    )
+    reach, run, side, psi, table, line = map(held, (reach, run, side, psi, table, line))
     maps = held(lax.all_to_all(sent, "gx", 0, 0))
     entries = call(
         scan_kernel,
-        near((slabs, 4 * QUAD, LANES), f32),
+        exchanged,
         [
             pltpu.VMEM((slabs, QUAD, LANES), f32),
             pltpu.VMEM((slabs + 1, QUAD, LANES), f32),
@@ -437,32 +494,33 @@
     back = held(lax.all_to_all(entries, "gx", 0, 0))
     partial_sums = call(
         lambda *refs: moments_kernel(groups, slabs, *refs),
-        near((groups, SENT_ROWS, cells), f32),
-        [
-            pltpu.VMEM((6 * cells, velocities), jnp.bfloat16),
-            pltpu.VMEM((LANES, velocities), f32),
-            pltpu.VMEM((8, cells), f32),
-        ],
+        near((groups, QUAD, SENT_PARTS * cells), f32),
+        [pltpu.VMEM((6 * cells, velocities), jnp.bfloat16)],
         reach,
         run,
         back,
-        velocity,
-        sign,
-        weight,
-        relax_rate,
+        psi,
+        table,
+        line,
     )
     parts = held(lax.all_to_all(partial_sums, "vert", 0, 0))
     new_state, new_macro = call(
         finish_kernel,
         (shape(state.shape, f32), shape(macro.shape, f32)),
-        [pltpu.VMEM((5 * cells_x, cells_y, LANES), f32), pltpu.VMEM((8, cells), f32)],
+        [
+            pltpu.VMEM(state.shape, f32),
+            pltpu.VMEM(macro.shape, f32),
+            pltpu.VMEM((5 * cells_x, cells_y, LANES), f32),
+            pltpu.VMEM((cells_y, velocities), f32),
+            pltpu.SemaphoreType.DMA((cells_x + 1,)),
+        ],
         parts,
         reach,
         run,
         back,
-        velocity,
-        sign,
-        relax_rate,
+        table,
+        line,
+        out_specs=(anywhere, anywhere),
     )
     return new_state, new_macro
 

time: 68.7 us -> 66.2 us (0.964)
  Pallas kernels: 5.82 us -> 4.35 us
  blocking collectives: 61.9 us -> 60.9 us
    pallas_call x4, Pallas kernels: 5.82 us -> 4.35 us  [call(): pl.pallas_call(body, out_shape=outs, scratch_shapes=scratch, interpret=IN...]
    all_to_all x1, blocking collectives: 33.6 us -> 32.6 us  [local(): parts = held(lax.all_to_all(partial_sums, 'vert', 0, 0))]
where the time goes in v3:
time: 66.2 us; the launch traced here: 65.9 us
  blocking collectives  60.9 us (92%)
  Pallas kernels  4.35 us (7%)
    all_to_all x1, blocking collectives, local(): parts = held(lax.all_to_all(partial_sums, 'vert', 0, 0))  32.6 us
    all_to_all x1, blocking collectives, local(): maps = held(lax.all_to_all(sent, 'gx', 0, 0))  15.9 us
    all_to_all x1, blocking collectives, local(): back = held(lax.all_to_all(entries, 'gx', 0, 0))  12.4 us
    pallas_call x4, Pallas kernels, call(): pl.pallas_call(body, out_shape=outs, scratch_shapes=scratch, interpret=IN...  4.35 us

profile of v3, /device:TPU:32, one launch (start us, length us, event | category | flops | bytes accessed | tf_op | source)
XLA Modules:
  0.0 65.9 jit_solution(3395083828275874807)
XLA Ops:
  0.6 1.8 %shard_map.95 = (f32[8,16,1024]{2,1,0:T(8,128)S(1)}, f32[8,16,1024]{2,1,0:T(8,128)S(1)}, f32[32,16,128]{2,1,0:T(8,128)S(1)}, f32[32,16,128]{2,1,0:T(8,128)S(1)},...) custom-call(f32[8,16,1024]{2,1,0:T(8,128)} %refs_0_.1, f32[5,8,16]{2,1,0:T(8,128)} %refs_1_.1, ...), custom_call_target="tpu_custom_call" | custom-call | tf_op jit(solution)/shard_map/pallas_call | solution.py:455
  2.5 15.9 %all_to_all.15.maps_ref = f32[32,16,128]{2,1,0:T(8,128)S(1)} all-to-all(f32[32,16,128]{2,1,0:T(8,128)S(1)} %get-tuple-element.11), channel_id=1, replica_groups=mesh['gx'=32,'vert'=16] {'gx'}, dimensions={0} | all-to-all | bytes 524288 | tf_op jit(solution)/shard_map/all_to_all | solution.py:483
  18.4 0.1 shard_map.96
  18.5 12.4 %all_to_all.16.refs_2_.back_ref = f32[32,16,128]{2,1,0:T(8,128)S(1)} all-to-all(f32[32,16,128]{2,1,0:T(8,128)S(1)} %shard_map.96), channel_id=1, replica_groups=mesh['gx'=32,'vert'=16] {'gx'}, dimensions={0} | all-to-all | bytes 524288 | tf_op jit(solution)/shard_map/all_to_all | solution.py:494
  30.9 0.9 %shard_map.97 = f32[16,4,896]{2,1,0:T(4,128)S(1)} custom-call(f32[8,16,1024]{2,1,0:T(8,128)S(1)} %get-tuple-element.9.refs_0_.reach_ref, f32[8,16,1024]{2,1,0:T(8,128)S(1)} %get-tuple-element.10.refs_1_.run_ref, f32[32,16,128]{2,1,0:T(8,128)S(1)} %all_to_all.16.refs_2_.back_ref, f32[32,1024]{1,0:T(8,128)S(1)} %get-tuple-element.13.refs_3_, ...), custom_call_target="tpu_custom_call" | custom-call | tf_op jit(solution)/shard_map/pallas_call | solution.py:455
  31.8 32.6 %all_to_all.17.parts_ref = f32[16,4,896]{2,1,0:T(4,128)S(1)} all-to-all(f32[16,4,896]{2,1,0:T(4,128)S(1)} %shard_map.97), channel_id=1, replica_groups=mesh['gx'=32,'vert'=16] {'vert'}, dimensions={0} | all-to-all | bytes 458752 | tf_op jit(solution)/shard_map/all_to_all | solution.py:506
  64.4 1.5 %shard_map.98 = (f32[8,16,1024]{2,1,0:T(8,128)}, f32[5,8,16]{2,1,0:T(8,128)}) custom-call(f32[16,4,896]{2,1,0:T(4,128)S(1)} %all_to_all.17.parts_ref, f32[8,16,1024]{2,1,0:T(8,128)S(1)} %get-tuple-element.9.refs_0_.reach_ref, f32[8,16,1024]{2,1,0:T(8,128)S(1)} %get-tuple-element.10.refs_1_.run_ref, f32[32,16,128]{2,1,0:T(8,128)S(1)} %all_to_all.16.refs_2_.back_ref, ...), custom_call_target="tpu_custom_call" | custom-call | tf_op jit(solution)/shard_map/pallas_call | solution.py:455

commit v4 on v3

--- a/solution.py
+++ b/solution.py
@@ -39,6 +39,7 @@
     wall_ref,
     pad_ref,
     spread_ref,
+    rows_ref,
     sems,
 ):
     fields, cells_x, cells_y = macro_ref.shape
@@ -67,12 +68,13 @@
         )
         for half in range(halves)
     ]
-    for copy in small + large:
+    for copy in large + small:
         copy.start()
     pad_ref[...] = jnp.zeros_like(pad_ref)
     psi_ref[...] = jnp.zeros_like(psi_ref)
     table_ref[...] = jnp.zeros_like(table_ref)
     line_ref[...] = jnp.zeros_like(line_ref)
+    rows_ref[...] = jnp.zeros_like(rows_ref)
     for copy in small:
         copy.wait()
     for k in range(fields):
@@ -87,6 +89,14 @@
     for x in range(cells_x):
         line_ref[0:1, x * cells_y : (x + 1) * cells_y] = relax_ref[x : x + 1, :]
     line_ref[0:1, :] = 0.2 / (1.0 + line_ref[0:1, :])
+    quads = cells_y // QUAD
+    for x in range(cells_x):
+        for quad in range(quads):
+            rows_ref[quad : quad + 1, x * QUAD : (x + 1) * QUAD] = relax_ref[
+                x : x + 1, quad * QUAD : (quad + 1) * QUAD
+            ]
+    rows_ref[quads : quads + 1, 0:cells_y] = relax_ref[0:1, :]
+    rows_ref[quads : quads + 1, cells_y : 2 * cells_y] = relax_ref[cells_x - 1 : cells_x, :]
 
     magnitude = velocity_ref[0:1, :]
     positive = sign_ref[...] == 1
@@ -168,55 +178,82 @@
             for part in range(8 // QUAD):
                 owner = (half * (8 // QUAD) + part) * tiles + tile
                 quad = slice(part * QUAD, (part + 1) * QUAD)
-                for slot, value in enumerate((products[last], runs[last], steps[0], gains[0])):
-                    sent_ref[owner, slot * QUAD : (slot + 1) * QUAD, :] = value[quad]
-                for slot, value in enumerate((fixed, unit, direction)):
+                for slot, value in enumerate((runs[last], gains[0])):
+                    for pair in range(QUAD // 2):
+                        start = (slot * (QUAD // 2) + pair) * LANES
+                        first = part * QUAD + 2 * pair
+                        sent_ref[owner, :, start : start + LANES] = value[first : first + 2]
+                index = half * (8 // QUAD) + part
+                sent_ref[owner, 0:1, QUAD * LANES :] = rows_ref[index : index + 1, :]
+                sent_ref[owner, 1:2, QUAD * LANES :] = rows_ref[quads : quads + 1, :]
+                for slot, value in enumerate((fixed, unit, direction, courant)):
                     side_ref[owner, slot * QUAD : (slot + 1) * QUAD, :] = value[quad]
 
 
-def scan_kernel(maps_ref, side_ref, sent_ref, entry_ref, near_ref):
+def scan_kernel(cells_x, maps_ref, side_ref, sent_ref, edges_ref, entry_ref, product_ref, gain_ref):
     slabs = maps_ref.shape[0]
     me = lax.axis_index("gx")
     side = side_ref[me]
     fixed = side[0:QUAD]
     unit = side[QUAD : 2 * QUAD]
     forward = side[2 * QUAD : 3 * QUAD] > 0.5
-    nothing = jnp.zeros_like(fixed)
+    courant = side[3 * QUAD : 4 * QUAD]
+    base = 1.0 + side[3 * QUAD : 3 * QUAD + 1]
+    power = courant
+    reach = 1
+    while reach < cells_x:
+        power = power * power
+        reach *= 2
+    edges_ref[...] = jnp.zeros_like(edges_ref)
+    below = jnp.maximum(me - 1, 0)
+    above = jnp.minimum(me + 1, slabs - 1)
+    edges_ref[0:1] = maps_ref[below, 1:2, QUAD * LANES :]
+    edges_ref[1:2] = maps_ref[above, 1:2, QUAD * LANES :]
+
+    def part(i, slot):
+        start = slot * (QUAD // 2) * LANES
+        return jnp.concatenate(
+            [
+                maps_ref[i, :, start + pair * LANES : start + (pair + 1) * LANES]
+                for pair in range(QUAD // 2)
+            ],
+            axis=0,
+        )
+
+    relax = jnp.concatenate(
+        [maps_ref[i, 0:1, QUAD * LANES :] for i in range(slabs)], axis=0
+    ).T
+    cells = cells_x * QUAD
+    for i in range(slabs):
+        divisors = base + jnp.broadcast_to(relax[0:cells, i : i + 1], (cells, LANES))
+        product = divisors[0:8]
+        for first in range(8, cells, 8):
+            product = product * divisors[first : first + 8]
+        product = product[0:QUAD] * product[QUAD:8]
+        product_ref[i] = power * (1.0 / product)
+        gain_ref[i] = part(i, 0)
     value = fixed
-    near_ref[0] = nothing
     for i in range(slabs - 1, -1, -1):
-        slab = maps_ref[i]
         entry_ref[i] = value
-        if i < slabs - 1:
-            near_ref[i + 1] = slab[2 * QUAD : 3 * QUAD] * value + slab[3 * QUAD : 4 * QUAD]
-        value = slab[0:QUAD] * value + slab[QUAD : 2 * QUAD]
-    near_ref[slabs] = slab[2 * QUAD : 3 * QUAD] * entry_ref[0] + slab[3 * QUAD : 4 * QUAD]
+        value = product_ref[i] * value + gain_ref[i]
     leaving = value
     value = fixed
     answer = unit
+    nothing = jnp.zeros_like(fixed)
     for i in range(slabs):
-        slab = maps_ref[i]
-        sent_ref[i, 0:QUAD] = jnp.where(forward, value, entry_ref[i])
-        sent_ref[i, QUAD : 2 * QUAD] = jnp.where(forward, answer, leaving)
-        value = slab[0:QUAD] * value + slab[QUAD : 2 * QUAD]
-        answer = slab[0:QUAD] * answer
-        upwind = near_ref[i] if i > 0 else nothing
-        if i < slabs - 1:
-            ahead = maps_ref[i + 1]
-            step = ahead[2 * QUAD : 3 * QUAD]
-            next_value = step * value + ahead[3 * QUAD : 4 * QUAD]
-            next_answer = step * answer
-        else:
-            next_value = nothing
-            next_answer = nothing
-        sent_ref[i, 2 * QUAD : 3 * QUAD] = jnp.where(forward, next_value, upwind)
-        sent_ref[i, 3 * QUAD : 4 * QUAD] = jnp.where(forward, next_answer, 0.0)
+        sent_ref[i, :, 0:LANES] = jnp.where(forward, value, entry_ref[i])
+        sent_ref[i, :, LANES : 2 * LANES] = jnp.where(forward, answer, leaving)
+        ahead = part(i + 1, 1) if i < slabs - 1 else nothing
+        behind = part(i - 1, 1) if i > 0 else nothing
+        sent_ref[i, :, 2 * LANES :] = jnp.where(forward, ahead, behind)
+        value = product_ref[i] * value + gain_ref[i]
+        answer = product_ref[i] * answer
 
 
 def whole_rows(back_ref, slot, tile, tiles, cells_y):
     return jnp.concatenate(
         [
-            back_ref[quad * tiles + tile, slot * QUAD : (slot + 1) * QUAD]
+            back_ref[quad * tiles + tile, :, slot * LANES : (slot + 1) * LANES]
             for quad in range(cells_y // QUAD)
         ],
         axis=0,
@@ -232,7 +269,17 @@
 
 
 def moments_kernel(
-    groups, slabs, reach_ref, run_ref, back_ref, psi_ref, table_ref, line_ref, sent_ref, left_ref
+    groups,
+    slabs,
+    reach_ref,
+    run_ref,
+    back_ref,
+    psi_ref,
+    table_ref,
+    line_ref,
+    edges_ref,
+    sent_ref,
+    left_ref,
 ):
     cells_x, cells_y, velocities = reach_ref.shape
     tiles = velocities // LANES
@@ -248,20 +295,32 @@
         left_ref[row : row + cells_y, lanes] = high
         left_ref[half + row : half + row + cells_y, lanes] = low
 
+    columns = edges_ref[...].T
+    relax_left = jnp.broadcast_to(columns[cells_y : 2 * cells_y, 0:1], (cells_y, LANES))
+    relax_right = jnp.broadcast_to(columns[0:cells_y, 1:2], (cells_y, LANES))
     for tile in range(tiles):
         lanes = slice(tile * LANES, (tile + 1) * LANES)
-        positive = table_ref[4:5, lanes] > 0.5
-        forward = jnp.broadcast_to(positive, (cells_y, LANES))
+        forward = jnp.broadcast_to(table_ref[4:5, lanes], (cells_y, LANES)) > 0.5
+        courant = jnp.broadcast_to(table_ref[5:6, lanes], (cells_y, LANES))
         entry = whole_rows(back_ref, 0, tile, tiles, cells_y)
         mixed = whole_rows(back_ref, 1, tile, tiles, cells_y)
-        near = whole_rows(back_ref, 2, tile, tiles, cells_y)
-        near_answer = whole_rows(back_ref, 3, tile, tiles, cells_y)
+        gain = whole_rows(back_ref, 2, tile, tiles, cells_y)
         answer = jnp.where(forward, mixed, 0.0)
         leaving = jnp.where(forward, 0.0, mixed)
         for x in range(cells_x):
             reach = reach_ref[x, :, lanes]
-            put(x * cells_y, reach * entry + run_ref[x, :, lanes], lanes)
+            value = reach * entry + run_ref[x, :, lanes]
+            put(x * cells_y, value, lanes)
             put(cells + x * cells_y, reach * answer, lanes)
+            if x == 0:
+                outgoing = value
+            if x == cells_x - 1:
+                outgoing = jnp.where(forward, value, outgoing)
+                outgoing_answer = reach * answer
+        decay = courant / (1.0 + courant + jnp.where(forward, relax_right, relax_left))
+        inside = jnp.where(forward, from_right, from_left)
+        near = (decay * outgoing + gain) * inside
+        near_answer = decay * outgoing_answer * inside
         row = 2 * cells
         put(row, jnp.where(forward, entry * from_left, near), lanes)
         put(row + cells_y, jnp.where(forward, near, entry * from_right), lanes)
@@ -458,14 +517,13 @@
 
     anywhere = pl.BlockSpec(memory_space=pl.ANY)
     sources = (state, macro, relax_rate, velocity, sign, weight, freestream, wall)
-    exchanged = near((slabs, 4 * QUAD, LANES), f32)
     reach, run, sent, side, psi, table, line = call(
         lambda *refs: maps_kernel(float(cells_x * slabs), groups, *refs),
         (
             near(state.shape, f32),
             near(state.shape, f32),
-            exchanged,
-            exchanged,
+            near((slabs, 2, (QUAD + 1) * LANES), f32),
+            near((slabs, 4 * QUAD, LANES), f32),
             near((32, velocities), f32),
             near((8, velocities), f32),
             near((8, cells), f32),
@@ -474,6 +532,7 @@
         + [
             pltpu.VMEM((fields * cells_x + 2 * cells_x, LANES), f32),
             pltpu.VMEM((fields * cells_x + cells_x + 1, cells_y, LANES), f32),
+            pltpu.VMEM((8, LANES), f32),
             pltpu.SemaphoreType.DMA((cells_y // 8 + 7,)),
         ],
         *sources,
@@ -481,16 +540,14 @@
     )
     reach, run, side, psi, table, line = map(held, (reach, run, side, psi, table, line))
     maps = held(lax.all_to_all(sent, "gx", 0, 0))
-    entries = call(
-        scan_kernel,
-        exchanged,
-        [
-            pltpu.VMEM((slabs, QUAD, LANES), f32),
-            pltpu.VMEM((slabs + 1, QUAD, LANES), f32),
-        ],
+    entries, edges = call(
+        lambda *refs: scan_kernel(cells_x, *refs),
+        (near((slabs, QUAD, 3 * LANES), f32), near((8, LANES), f32)),
+        [pltpu.VMEM((slabs, QUAD, LANES), f32)] * 3,
         maps,
         side,
     )
+    edges = held(edges)
     back = held(lax.all_to_all(entries, "gx", 0, 0))
     partial_sums = call(
         lambda *refs: moments_kernel(groups, slabs, *refs),
@@ -502,6 +559,7 @@
         psi,
         table,
         line,
+        edges,
     )
     parts = held(lax.all_to_all(partial_sums, "vert", 0, 0))
     new_state, new_macro = call(

time: 66.2 us -> 65.2 us (0.985)
  blocking collectives: 60.9 us -> 59.4 us
    all_to_all x1, blocking collectives: 15.9 us -> 15.1 us  [local(): maps = held(lax.all_to_all(sent, 'gx', 0, 0))]
    all_to_all x1, blocking collectives: 12.4 us -> 11.7 us  [local(): back = held(lax.all_to_all(entries, 'gx', 0, 0))]
where the time goes in v4:
time: 65.2 us; the launch traced here: 65 us
  blocking collectives  59.4 us (91%)
  Pallas kernels  4.98 us (8%)
  between operations  0.66 us (1%)
    all_to_all x1, blocking collectives, local(): parts = held(lax.all_to_all(partial_sums, 'vert', 0, 0))  32.6 us
    all_to_all x1, blocking collectives, local(): maps = held(lax.all_to_all(sent, 'gx', 0, 0))  15.1 us
    all_to_all x1, blocking collectives, local(): back = held(lax.all_to_all(entries, 'gx', 0, 0))  11.7 us
    pallas_call x4, Pallas kernels, call(): pl.pallas_call(body, out_shape=outs, scratch_shapes=scratch, interpret=IN...  4.98 us

profile of v4, /device:TPU:32, one launch (start us, length us, event | category | flops | bytes accessed | tf_op | source)
XLA Modules:
  0.0 65.0 jit_solution(1388077906882956823)
XLA Ops:
  0.6 2.1 %shard_map.95 = (f32[8,16,1024]{2,1,0:T(8,128)S(1)}, f32[8,16,1024]{2,1,0:T(8,128)S(1)}, f32[32,2,640]{2,1,0:T(2,128)S(1)}, f32[32,16,128]{2,1,0:T(8,128)S(1)}, ...) custom-call(f32[8,16,1024]{2,1,0:T(8,128)} %refs_0_.1, f32[5,8,16]{2,1,0:T(8,128)} %refs_1_.1, ...), custom_call_target="tpu_custom_call" | custom-call | tf_op jit(solution)/shard_map/pallas_call | solution.py:514
  2.7 15.1 %all_to_all.15.refs_0_ = f32[32,2,640]{2,1,0:T(2,128)S(1)} all-to-all(f32[32,2,640]{2,1,0:T(2,128)S(1)} %get-tuple-element.13), channel_id=1, replica_groups=mesh['gx'=32,'vert'=16] {'gx'}, dimensions={0} | all-to-all | bytes 327680 | tf_op jit(solution)/shard_map/all_to_all | solution.py:542
  17.8 0.5 shard_map.96
  18.3 11.7 %all_to_all.16.refs_2_.back_ref = f32[32,4,384]{2,1,0:T(4,128)S(1)} all-to-all(f32[32,4,384]{2,1,0:T(4,128)S(1)} %get-tuple-element.15), channel_id=1, replica_groups=mesh['gx'=32,'vert'=16] {'gx'}, dimensions={0} | all-to-all | bytes 393216 | tf_op jit(solution)/shard_map/all_to_all | solution.py:551
  30.0 0.9 %shard_map.97 = f32[16,4,896]{2,1,0:T(4,128)S(1)} custom-call(f32[8,16,1024]{2,1,0:T(8,128)S(1)} %get-tuple-element.11.refs_0_.reach_ref, f32[8,16,1024]{2,1,0:T(8,128)S(1)} %get-tuple-element.12.refs_1_.run_ref, f32[32,4,384]{2,1,0:T(4,128)S(1)} %all_to_all.16.refs_2_.back_ref, f32[32,1024]{1,0:T(8,128)S(1)} %get-tuple-element.16.refs_3_, ...), custom_call_target="tpu_custom_call" | custom-call | tf_op jit(solution)/shard_map/pallas_call | solution.py:514
  30.9 32.6 %all_to_all.17.parts_ref = f32[16,4,896]{2,1,0:T(4,128)S(1)} all-to-all(f32[16,4,896]{2,1,0:T(4,128)S(1)} %shard_map.97), channel_id=1, replica_groups=mesh['gx'=32,'vert'=16] {'vert'}, dimensions={0} | all-to-all | bytes 458752 | tf_op jit(solution)/shard_map/all_to_all | solution.py:564
  63.5 1.5 %shard_map.98 = (f32[8,16,1024]{2,1,0:T(8,128)}, f32[5,8,16]{2,1,0:T(8,128)}) custom-call(f32[16,4,896]{2,1,0:T(4,128)S(1)} %all_to_all.17.parts_ref, f32[8,16,1024]{2,1,0:T(8,128)S(1)} %get-tuple-element.11.refs_0_.reach_ref, f32[8,16,1024]{2,1,0:T(8,128)S(1)} %get-tuple-element.12.refs_1_.run_ref, f32[32,4,384]{2,1,0:T(4,128)S(1)} %all_to_all.16.refs_2_.back_ref, ...), custom_call_target="tpu_custom_call" | custom-call | tf_op jit(solution)/shard_map/pallas_call | solution.py:514

commit v5 on v4

--- a/solution.py
+++ b/solution.py
@@ -9,6 +9,26 @@
 QUAD = 4
 SENT_PARTS = 7
 INTERPRET = False
+
+
+def left_parts(value):
+    high = value.astype(jnp.bfloat16).astype(jnp.float32)
+    return jnp.concatenate([high, value - high, high, jnp.zeros_like(high)], axis=0).astype(
+        jnp.bfloat16
+    )
+
+
+def right_parts(value):
+    high = value.astype(jnp.bfloat16).astype(jnp.float32)
+    return jnp.concatenate([high, high, value - high, jnp.zeros_like(high)], axis=0).astype(
+        jnp.bfloat16
+    )
+
+
+def columns_product(left, right):
+    return lax.dot_general(
+        left, right, (((0,), (0,)), ((), ())), preferred_element_type=jnp.float32
+    )
 
 
 def maps_kernel(
@@ -27,6 +47,7 @@
     sent_ref,
     side_ref,
     psi_ref,
+    phi_ref,
     table_ref,
     line_ref,
     state_ref,
@@ -37,9 +58,11 @@
     weight_ref,
     free_ref,
     wall_ref,
-    pad_ref,
+    cells_ref,
+    basis_ref,
+    moment_ref,
+    equil_ref,
     spread_ref,
-    rows_ref,
     sems,
 ):
     fields, cells_x, cells_y = macro_ref.shape
@@ -70,33 +93,23 @@
     ]
     for copy in large + small:
         copy.start()
-    pad_ref[...] = jnp.zeros_like(pad_ref)
-    psi_ref[...] = jnp.zeros_like(psi_ref)
-    table_ref[...] = jnp.zeros_like(table_ref)
-    line_ref[...] = jnp.zeros_like(line_ref)
-    rows_ref[...] = jnp.zeros_like(rows_ref)
+    for ref in (cells_ref, basis_ref, moment_ref, table_ref, line_ref):
+        ref[...] = jnp.zeros_like(ref)
     for copy in small:
         copy.wait()
-    for k in range(fields):
-        pad_ref[k * cells_x : (k + 1) * cells_x, 0:cells_y] = macro_ref[k]
-    base_row = fields * cells_x
-    pad_ref[base_row : base_row + cells_x, 0:cells_y] = relax_ref[...]
-    wall_row = base_row + cells_x
-    pad_ref[wall_row : wall_row + 1, 0:cells_y] = (wall_ref[...] == 1).astype(jnp.float32)
-    columns = pad_ref[...].T
-    for c in range(wall_row + 1):
-        spread_ref[c] = jnp.broadcast_to(columns[0:cells_y, c : c + 1], (cells_y, LANES))
     for x in range(cells_x):
-        line_ref[0:1, x * cells_y : (x + 1) * cells_y] = relax_ref[x : x + 1, :]
-    line_ref[0:1, :] = 0.2 / (1.0 + line_ref[0:1, :])
-    quads = cells_y // QUAD
+        where = slice(x * cells_y, (x + 1) * cells_y)
+        cells_ref[0:fields, where] = macro_ref[:, x, :]
+        line_ref[0:1, where] = relax_ref[x : x + 1, :]
+    line_ref[1:2, 0:cells_y] = (wall_ref[...] == 1).astype(jnp.float32)
+    columns = line_ref[...].T
     for x in range(cells_x):
-        for quad in range(quads):
-            rows_ref[quad : quad + 1, x * QUAD : (x + 1) * QUAD] = relax_ref[
-                x : x + 1, quad * QUAD : (quad + 1) * QUAD
-            ]
-    rows_ref[quads : quads + 1, 0:cells_y] = relax_ref[0:1, :]
-    rows_ref[quads : quads + 1, cells_y : 2 * cells_y] = relax_ref[cells_x - 1 : cells_x, :]
+        spread_ref[x] = jnp.broadcast_to(
+            columns[x * cells_y : (x + 1) * cells_y, 0:1], (cells_y, LANES)
+        )
+    spread_ref[cells_x] = jnp.broadcast_to(columns[0:cells_y, 1:2], (cells_y, LANES))
+    relax_row = line_ref[0:1, :]
+    line_ref[2:3, :] = 0.2 / (1.0 + relax_row)
 
     magnitude = velocity_ref[0:1, :]
     positive = sign_ref[...] == 1
@@ -104,17 +117,13 @@
     cy = velocity_ref[1:2, :]
     cz = velocity_ref[2:3, :]
     square = cx * cx + cy * cy + cz * cz
-    for k, row in enumerate(
-        (
-            2.0 * cx,
-            2.0 * cy,
-            2.0 * cz,
-            square - 1.5,
-            jnp.where(positive, 1.0, 0.0),
-            total_cells * magnitude,
-        )
-    ):
-        table_ref[k : k + 1, :] = row
+    for k, row in enumerate((jnp.ones_like(cx), 2.0 * cx, 2.0 * cy, 2.0 * cz, square - 1.5)):
+        basis_ref[k : k + 1, :] = row
+    table_ref[0:1, :] = jnp.where(positive, 1.0, 0.0)
+    table_ref[1:2, :] = total_cells * magnitude
+    phi = right_parts(basis_ref[...])
+    phi_ref[...] = phi
+    equil_ref[...] = columns_product(left_parts(cells_ref[...]), phi)
     weight = weight_ref[...] / (velocities * groups)
     heat = 0.2 * (square - 2.5)
     for k, row in enumerate(
@@ -135,10 +144,10 @@
             magnitude,
         )
     ):
-        value = weight * row
-        high = value.astype(jnp.bfloat16).astype(jnp.float32)
-        psi_ref[k : k + 1, :] = high
-        psi_ref[16 + k : 17 + k, :] = value - high
+        moment_ref[k : k + 1, :] = weight * row
+    high = moment_ref[...].astype(jnp.bfloat16)
+    psi_ref[0:16] = high
+    psi_ref[16:32] = (moment_ref[...] - high.astype(jnp.float32)).astype(jnp.bfloat16)
 
     last = cells_x - 1
     for half in range(halves):
@@ -146,17 +155,15 @@
         rows = slice(half * 8, half * 8 + 8)
         for tile in range(tiles):
             lanes = slice(tile * LANES, (tile + 1) * LANES)
-            forward = jnp.broadcast_to(table_ref[4:5, lanes], (8, LANES)) > 0.5
-            courant = jnp.broadcast_to(table_ref[5:6, lanes], (8, LANES))
+            forward = jnp.broadcast_to(table_ref[0:1, lanes], (8, LANES)) > 0.5
+            courant = jnp.broadcast_to(table_ref[1:2, lanes], (8, LANES))
             base = 1.0 + courant
-            basis = [jnp.broadcast_to(table_ref[k : k + 1, lanes], (8, LANES)) for k in range(4)]
             decay = []
             driven = []
             for x in range(cells_x):
-                relax = spread_ref[base_row + x, rows]
-                equil = spread_ref[x, rows]
-                for k in range(1, fields):
-                    equil = equil + spread_ref[k * cells_x + x, rows] * basis[k - 1]
+                relax = spread_ref[x, rows]
+                first = x * cells_y + half * 8
+                equil = equil_ref[first : first + 8, lanes]
                 inverse = 1.0 / (base + relax)
                 decay.append(courant * inverse)
                 driven.append((state_ref[x, rows, lanes] + relax * equil) * inverse)
@@ -170,7 +177,7 @@
             for x in range(cells_x):
                 reach_ref[x, rows, lanes] = jnp.where(forward, products[x], products[last - x])
                 run_ref[x, rows, lanes] = jnp.where(forward, runs[x], runs[last - x])
-            wall = spread_ref[wall_row, rows] > 0.5
+            wall = spread_ref[cells_x, rows] > 0.5
             diffuse = jnp.logical_and(forward, wall)
             fixed = jnp.where(diffuse, 0.0, free_ref[rows, lanes])
             unit = jnp.where(diffuse, 1.0, 0.0)
@@ -183,9 +190,7 @@
                         start = (slot * (QUAD // 2) + pair) * LANES
                         first = part * QUAD + 2 * pair
                         sent_ref[owner, :, start : start + LANES] = value[first : first + 2]
-                index = half * (8 // QUAD) + part
-                sent_ref[owner, 0:1, QUAD * LANES :] = rows_ref[index : index + 1, :]
-                sent_ref[owner, 1:2, QUAD * LANES :] = rows_ref[quads : quads + 1, :]
+                sent_ref[owner, 0:1, QUAD * LANES :] = relax_row
                 for slot, value in enumerate((fixed, unit, direction, courant)):
                     side_ref[owner, slot * QUAD : (slot + 1) * QUAD, :] = value[quad]
 
@@ -207,8 +212,8 @@
     edges_ref[...] = jnp.zeros_like(edges_ref)
     below = jnp.maximum(me - 1, 0)
     above = jnp.minimum(me + 1, slabs - 1)
-    edges_ref[0:1] = maps_ref[below, 1:2, QUAD * LANES :]
-    edges_ref[1:2] = maps_ref[above, 1:2, QUAD * LANES :]
+    edges_ref[0:1] = maps_ref[below, 0:1, QUAD * LANES :]
+    edges_ref[1:2] = maps_ref[above, 0:1, QUAD * LANES :]
 
     def part(i, slot):
         start = slot * (QUAD // 2) * LANES
@@ -223,9 +228,20 @@
     relax = jnp.concatenate(
         [maps_ref[i, 0:1, QUAD * LANES :] for i in range(slabs)], axis=0
     ).T
+    cells_y = relax.shape[0] // cells_x
+    quads = cells_y // QUAD
+    index = me // (slabs // quads)
+    high = index // 2 == 1
+    odd = index % 2 == 1
+    picked = []
+    for x in range(cells_x):
+        rows = relax[x * cells_y : (x + 1) * cells_y]
+        rows = jnp.where(high, rows[8:16], rows[0:8])
+        picked.append(jnp.where(odd, rows[QUAD:8], rows[0:QUAD]))
+    relax = jnp.concatenate(picked, axis=0)
     cells = cells_x * QUAD
     for i in range(slabs):
-        divisors = base + jnp.broadcast_to(relax[0:cells, i : i + 1], (cells, LANES))
+        divisors = base + jnp.broadcast_to(relax[:, i : i + 1], (cells, LANES))
         product = divisors[0:8]
         for first in range(8, cells, 8):
             product = product * divisors[first : first + 8]
@@ -296,12 +312,12 @@
         left_ref[half + row : half + row + cells_y, lanes] = low
 
     columns = edges_ref[...].T
-    relax_left = jnp.broadcast_to(columns[cells_y : 2 * cells_y, 0:1], (cells_y, LANES))
+    relax_left = jnp.broadcast_to(columns[cells - cells_y : cells, 0:1], (cells_y, LANES))
     relax_right = jnp.broadcast_to(columns[0:cells_y, 1:2], (cells_y, LANES))
     for tile in range(tiles):
         lanes = slice(tile * LANES, (tile + 1) * LANES)
-        forward = jnp.broadcast_to(table_ref[4:5, lanes], (cells_y, LANES)) > 0.5
-        courant = jnp.broadcast_to(table_ref[5:6, lanes], (cells_y, LANES))
+        forward = jnp.broadcast_to(table_ref[0:1, lanes], (cells_y, LANES)) > 0.5
+        courant = jnp.broadcast_to(table_ref[1:2, lanes], (cells_y, LANES))
         entry = whole_rows(back_ref, 0, tile, tiles, cells_y)
         mixed = whole_rows(back_ref, 1, tile, tiles, cells_y)
         gain = whole_rows(back_ref, 2, tile, tiles, cells_y)
@@ -332,18 +348,18 @@
         put(row + 7 * cells_y, jnp.zeros_like(entry), lanes)
 
     product = lax.dot_general(
+        psi_ref[...],
         left_ref[...],
-        psi_ref[...].astype(jnp.bfloat16),
         (((1,), (1,)), ((), ())),
         preferred_element_type=jnp.float32,
     )
-    upper = product[0:half]
-    total = upper[:, 0:16] + upper[:, 16:32] + product[half:, 0:16]
-    fixed = total[0:cells].T
-    answer = total[cells : 2 * cells].T
-    edges = total[2 * cells : 3 * cells].T
-
-    spread = line_ref[0:1, :]
+    upper = product[:, 0:half]
+    total = upper[0:16] + upper[16:32] + product[0:16, half:]
+    fixed = total[:, 0:cells]
+    answer = total[:, cells : 2 * cells]
+    edges = total[:, 2 * cells : 3 * cells]
+
+    spread = line_ref[2:3, :]
     lane = lax.broadcasted_iota(jnp.int32, (16, cells), 1)
 
     def along(m, at_left, at_right):
@@ -408,13 +424,14 @@
     reach_ref,
     run_ref,
     back_ref,
+    phi_ref,
     table_ref,
     line_ref,
     state_hbm,
     macro_hbm,
     state_ref,
     macro_ref,
-    spread_ref,
+    change_ref,
     entry_ref,
     sems,
 ):
@@ -451,23 +468,22 @@
         ],
         axis=0,
     )
-    spread = line_ref[0:1, :]
+    spread = line_ref[2:3, :]
     change = total[5:10] + rho * total[19:24] + spread * (yp + ym)[2:7] - 0.25 * flow
     updated = total[0:5] + answer[2:7] + change
     for x in range(cells_x):
         macro_ref[:, x, :] = updated[:, x * cells_y : (x + 1) * cells_y]
     macro_copy = pltpu.make_async_copy(macro_ref, macro_hbm, sems.at[cells_x])
     macro_copy.start()
-    columns = jnp.concatenate([change, rho, jnp.zeros((2, cells), jnp.float32)], axis=0).T
-    for x in range(cells_x):
-        for k in range(5):
-            spread_ref[k * cells_x + x] = jnp.broadcast_to(
-                columns[x * cells_y : (x + 1) * cells_y, k : k + 1], (cells_y, LANES)
-            )
-    density = jnp.broadcast_to(columns[0:cells_y, 5:6], (cells_y, LANES))
+    spare = jnp.zeros((3, cells), jnp.float32)
+    change_ref[...] = columns_product(
+        left_parts(jnp.concatenate([change, spare], axis=0)), phi_ref[...]
+    )
+    columns = jnp.broadcast_to(rho, (8, cells)).T
+    density = jnp.broadcast_to(columns[0:cells_y, 0:1], (cells_y, LANES))
     for tile in range(tiles):
         lanes = slice(tile * LANES, (tile + 1) * LANES)
-        forward = jnp.broadcast_to(table_ref[4:5, lanes], (cells_y, LANES)) > 0.5
+        forward = jnp.broadcast_to(table_ref[0:1, lanes], (cells_y, LANES)) > 0.5
         entry = whole_rows(back_ref, 0, tile, tiles, cells_y)
         mixed = whole_rows(back_ref, 1, tile, tiles, cells_y)
         entry_ref[:, lanes] = entry + jnp.where(forward, density * mixed, 0.0)
@@ -476,12 +492,10 @@
     for first in range(0, cells_x, span):
         for tile in range(tiles):
             lanes = slice(tile * LANES, (tile + 1) * LANES)
-            basis = [table_ref[k : k + 1, lanes] for k in range(4)]
             entry = entry_ref[:, lanes]
             for x in range(first, first + span):
-                value = reach_ref[x, :, lanes] * entry + run_ref[x, :, lanes] + spread_ref[x]
-                for k in range(1, 5):
-                    value = value + spread_ref[k * cells_x + x] * basis[k - 1]
+                change = change_ref[x * cells_y : (x + 1) * cells_y, lanes]
+                value = reach_ref[x, :, lanes] * entry + run_ref[x, :, lanes] + change
                 state_ref[x, :, lanes] = value
         copy = pltpu.make_async_copy(
             state_ref.at[pl.ds(first, span)], state_hbm.at[pl.ds(first, span)], sems.at[first]
@@ -517,28 +531,32 @@
 
     anywhere = pl.BlockSpec(memory_space=pl.ANY)
     sources = (state, macro, relax_rate, velocity, sign, weight, freestream, wall)
-    reach, run, sent, side, psi, table, line = call(
+    reach, run, sent, side, psi, phi, table, line = call(
         lambda *refs: maps_kernel(float(cells_x * slabs), groups, *refs),
         (
             near(state.shape, f32),
             near(state.shape, f32),
             near((slabs, 2, (QUAD + 1) * LANES), f32),
             near((slabs, 4 * QUAD, LANES), f32),
-            near((32, velocities), f32),
+            near((32, velocities), jnp.bfloat16),
+            near((32, velocities), jnp.bfloat16),
             near((8, velocities), f32),
             near((8, cells), f32),
         ),
         [pltpu.VMEM(value.shape, value.dtype) for value in sources]
         + [
-            pltpu.VMEM((fields * cells_x + 2 * cells_x, LANES), f32),
-            pltpu.VMEM((fields * cells_x + cells_x + 1, cells_y, LANES), f32),
-            pltpu.VMEM((8, LANES), f32),
+            pltpu.VMEM((8, cells), f32),
+            pltpu.VMEM((8, velocities), f32),
+            pltpu.VMEM((16, velocities), f32),
+            pltpu.VMEM((cells, velocities), f32),
+            pltpu.VMEM((cells_x + 1, cells_y, LANES), f32),
             pltpu.SemaphoreType.DMA((cells_y // 8 + 7,)),
         ],
         *sources,
         in_specs=[anywhere] * len(sources),
     )
-    reach, run, side, psi, table, line = map(held, (reach, run, side, psi, table, line))
+    reach, run, side = map(held, (reach, run, side))
+    psi, phi, table, line = map(held, (psi, phi, table, line))
     maps = held(lax.all_to_all(sent, "gx", 0, 0))
     entries, edges = call(
         lambda *refs: scan_kernel(cells_x, *refs),
@@ -568,7 +586,7 @@
         [
             pltpu.VMEM(state.shape, f32),
             pltpu.VMEM(macro.shape, f32),
-            pltpu.VMEM((5 * cells_x, cells_y, LANES), f32),
+            pltpu.VMEM((cells, velocities), f32),
             pltpu.VMEM((cells_y, velocities), f32),
             pltpu.SemaphoreType.DMA((cells_x + 1,)),
         ],
@@ -576,6 +594,7 @@
         reach,
         run,
         back,
+        phi,
         table,
         line,
         out_specs=(anywhere, anywhere),

time: 65.2 us -> 64.9 us (level)
  no operation moved by 1% of the time
where the time goes in v5:
time: 64.9 us; the launch traced here: 64.7 us
  blocking collectives  59.4 us (92%)
  Pallas kernels  4.62 us (7%)
  between operations  0.66 us (1%)
    all_to_all x1, blocking collectives, local(): parts = held(lax.all_to_all(partial_sums, 'vert', 0, 0))  32.6 us
    all_to_all x1, blocking collectives, local(): maps = held(lax.all_to_all(sent, 'gx', 0, 0))  15.1 us
    all_to_all x1, blocking collectives, local(): back = held(lax.all_to_all(entries, 'gx', 0, 0))  11.7 us
    pallas_call x4, Pallas kernels, call(): pl.pallas_call(body, out_shape=outs, scratch_shapes=scratch, interpret=IN...  4.62 us

profile of v5, /device:TPU:32, one launch (start us, length us, event | category | flops | bytes accessed | tf_op | source)
XLA Modules:
  0.0 64.7 jit_solution(5970411993477745862)
XLA Ops:
  0.6 1.8 %shard_map.95 = (f32[8,16,1024]{2,1,0:T(8,128)S(1)}, f32[8,16,1024]{2,1,0:T(8,128)S(1)}, f32[32,2,640]{2,1,0:T(2,128)S(1)}, f32[32,16,128]{2,1,0:T(8,128)S(1)}, ...) custom-call(f32[8,16,1024]{2,1,0:T(8,128)} %refs_0_.1, ...), custom_call_target="tpu_custom_call" | custom-call | tf_op jit(solution)/shard_map/pallas_call | solution.py:528
  2.5 15.1 %all_to_all.15.refs_0_ = f32[32,2,640]{2,1,0:T(2,128)S(1)} all-to-all(f32[32,2,640]{2,1,0:T(2,128)S(1)} %get-tuple-element.14), channel_id=1, replica_groups=mesh['gx'=32,'vert'=16] {'gx'}, dimensions={0} | all-to-all | bytes 327680 | tf_op jit(solution)/shard_map/all_to_all | solution.py:560
  17.6 0.5 shard_map.96
  18.1 11.7 %all_to_all.16.refs_2_.back_ref = f32[32,4,384]{2,1,0:T(4,128)S(1)} all-to-all(f32[32,4,384]{2,1,0:T(4,128)S(1)} %get-tuple-element.16), channel_id=1, replica_groups=mesh['gx'=32,'vert'=16] {'gx'}, dimensions={0} | all-to-all | bytes 393216 | tf_op jit(solution)/shard_map/all_to_all | solution.py:569
  29.8 0.8 %shard_map.97 = f32[16,4,896]{2,1,0:T(4,128)S(1)} custom-call(f32[8,16,1024]{2,1,0:T(8,128)S(1)} %get-tuple-element.12.refs_0_.reach_ref, f32[8,16,1024]{2,1,0:T(8,128)S(1)} %get-tuple-element.13.refs_1_.run_ref, f32[32,4,384]{2,1,0:T(4,128)S(1)} %all_to_all.16.refs_2_.back_ref, bf16[32,1024]{1,0:T(8,128)(2,1)S(1)} %get-tuple-element.17.refs_3_, ...), custom_call_target="tpu_custom_call" | custom-call | tf_op jit(solution)/shard_map/pallas_call | solution.py:528
  30.6 32.6 %all_to_all.17.parts_ref = f32[16,4,896]{2,1,0:T(4,128)S(1)} all-to-all(f32[16,4,896]{2,1,0:T(4,128)S(1)} %shard_map.97), channel_id=1, replica_groups=mesh['gx'=32,'vert'=16] {'vert'}, dimensions={0} | all-to-all | bytes 458752 | tf_op jit(solution)/shard_map/all_to_all | solution.py:582
  63.2 1.5 %shard_map.98 = (f32[8,16,1024]{2,1,0:T(8,128)}, f32[5,8,16]{2,1,0:T(8,128)}) custom-call(f32[16,4,896]{2,1,0:T(4,128)S(1)} %all_to_all.17.parts_ref, f32[8,16,1024]{2,1,0:T(8,128)S(1)} %get-tuple-element.12.refs_0_.reach_ref, f32[8,16,1024]{2,1,0:T(8,128)S(1)} %get-tuple-element.13.refs_1_.run_ref, f32[32,4,384]{2,1,0:T(4,128)S(1)} %all_to_all.16.refs_2_.back_ref, ...), custom_call_target="tpu_custom_call" | custom-call | tf_op jit(solution)/shard_map/pallas_call | solution.py:528

commit v6 on v5

--- a/solution.py
+++ b/solution.py
@@ -7,6 +7,7 @@
 
 LANES = 128
 QUAD = 4
+EDGE_ROWS = (0, 1, 2, 3, 4, 5, 6, 8, 10)
 SENT_PARTS = 7
 INTERPRET = False
 
@@ -29,6 +30,27 @@
     return lax.dot_general(
         left, right, (((0,), (0,)), ((), ())), preferred_element_type=jnp.float32
     )
+
+
+def split_put(ref, row, lanes, value):
+    half = ref.shape[0] // 2
+    count = value.shape[0]
+    high = value.astype(jnp.bfloat16)
+    ref[row : row + count, lanes] = high
+    ref[half + row : half + row + count, lanes] = (value - high.astype(jnp.float32)).astype(
+        jnp.bfloat16
+    )
+
+
+def split_moments(psi_ref, left_ref):
+    half = left_ref.shape[0] // 2
+    product = lax.dot_general(
+        psi_ref[...],
+        left_ref[...],
+        (((1,), (1,)), ((), ())),
+        preferred_element_type=jnp.float32,
+    )
+    return product[0:16, 0:half] + product[16:32, 0:half] + product[0:16, half:]
 
 
 def maps_kernel(
@@ -63,6 +85,8 @@
     moment_ref,
     equil_ref,
     spread_ref,
+    left_ref,
+    message_ref,
     sems,
 ):
     fields, cells_x, cells_y = macro_ref.shape
@@ -93,7 +117,7 @@
     ]
     for copy in large + small:
         copy.start()
-    for ref in (cells_ref, basis_ref, moment_ref, table_ref, line_ref):
+    for ref in (cells_ref, basis_ref, moment_ref, table_ref, line_ref, message_ref, left_ref):
         ref[...] = jnp.zeros_like(ref)
     for copy in small:
         copy.wait()
@@ -182,20 +206,30 @@
             fixed = jnp.where(diffuse, 0.0, free_ref[rows, lanes])
             unit = jnp.where(diffuse, 1.0, 0.0)
             direction = jnp.where(forward, 1.0, 0.0)
+            first_gain = gains[0]
+            outward = jnp.where(forward, first_gain, 0.0)
+            split_put(left_ref, half * 8, lanes, outward)
+            split_put(left_ref, cells_y + half * 8, lanes, first_gain - outward)
             for part in range(8 // QUAD):
                 owner = (half * (8 // QUAD) + part) * tiles + tile
                 quad = slice(part * QUAD, (part + 1) * QUAD)
-                for slot, value in enumerate((runs[last], gains[0])):
-                    for pair in range(QUAD // 2):
-                        start = (slot * (QUAD // 2) + pair) * LANES
-                        first = part * QUAD + 2 * pair
-                        sent_ref[owner, :, start : start + LANES] = value[first : first + 2]
-                sent_ref[owner, 0:1, QUAD * LANES :] = relax_row
+                sent_ref[owner, 0:QUAD, :] = runs[last][quad]
                 for slot, value in enumerate((fixed, unit, direction, courant)):
                     side_ref[owner, slot * QUAD : (slot + 1) * QUAD, :] = value[quad]
-
-
-def scan_kernel(cells_x, maps_ref, side_ref, sent_ref, edges_ref, entry_ref, product_ref, gain_ref):
+    message_ref[0:1, :] = relax_row
+    edge_moments = split_moments(psi_ref, left_ref)
+    for n, k in enumerate(EDGE_ROWS):
+        row = 1 + n // QUAD
+        start = (n % QUAD) * 2 * cells_y
+        message_ref[row : row + 1, start : start + 2 * cells_y] = edge_moments[
+            k : k + 1, 0 : 2 * cells_y
+        ]
+    message = message_ref[0:QUAD]
+    for owner in range(sent_ref.shape[0]):
+        sent_ref[owner, QUAD : 2 * QUAD, :] = message
+
+
+def scan_kernel(cells_x, maps_ref, side_ref, sent_ref, edges_ref, entry_ref, product_ref):
     slabs = maps_ref.shape[0]
     me = lax.axis_index("gx")
     side = side_ref[me]
@@ -209,25 +243,11 @@
     while reach < cells_x:
         power = power * power
         reach *= 2
-    edges_ref[...] = jnp.zeros_like(edges_ref)
     below = jnp.maximum(me - 1, 0)
     above = jnp.minimum(me + 1, slabs - 1)
-    edges_ref[0:1] = maps_ref[below, 0:1, QUAD * LANES :]
-    edges_ref[1:2] = maps_ref[above, 0:1, QUAD * LANES :]
-
-    def part(i, slot):
-        start = slot * (QUAD // 2) * LANES
-        return jnp.concatenate(
-            [
-                maps_ref[i, :, start + pair * LANES : start + (pair + 1) * LANES]
-                for pair in range(QUAD // 2)
-            ],
-            axis=0,
-        )
-
-    relax = jnp.concatenate(
-        [maps_ref[i, 0:1, QUAD * LANES :] for i in range(slabs)], axis=0
-    ).T
+    edges_ref[0:QUAD] = maps_ref[below, QUAD : 2 * QUAD]
+    edges_ref[QUAD : 2 * QUAD] = maps_ref[above, QUAD : 2 * QUAD]
+    relax = jnp.concatenate([maps_ref[i, QUAD : QUAD + 1] for i in range(slabs)], axis=0).T
     cells_y = relax.shape[0] // cells_x
     quads = cells_y // QUAD
     index = me // (slabs // quads)
@@ -247,29 +267,24 @@
             product = product * divisors[first : first + 8]
         product = product[0:QUAD] * product[QUAD:8]
         product_ref[i] = power * (1.0 / product)
-        gain_ref[i] = part(i, 0)
     value = fixed
     for i in range(slabs - 1, -1, -1):
         entry_ref[i] = value
-        value = product_ref[i] * value + gain_ref[i]
+        value = product_ref[i] * value + maps_ref[i, 0:QUAD]
     leaving = value
     value = fixed
     answer = unit
-    nothing = jnp.zeros_like(fixed)
     for i in range(slabs):
-        sent_ref[i, :, 0:LANES] = jnp.where(forward, value, entry_ref[i])
-        sent_ref[i, :, LANES : 2 * LANES] = jnp.where(forward, answer, leaving)
-        ahead = part(i + 1, 1) if i < slabs - 1 else nothing
-        behind = part(i - 1, 1) if i > 0 else nothing
-        sent_ref[i, :, 2 * LANES :] = jnp.where(forward, ahead, behind)
-        value = product_ref[i] * value + gain_ref[i]
+        sent_ref[i, 0:QUAD] = jnp.where(forward, value, entry_ref[i])
+        sent_ref[i, QUAD : 2 * QUAD] = jnp.where(forward, answer, leaving)
+        value = product_ref[i] * value + maps_ref[i, 0:QUAD]
         answer = product_ref[i] * answer
 
 
 def whole_rows(back_ref, slot, tile, tiles, cells_y):
     return jnp.concatenate(
         [
-            back_ref[quad * tiles + tile, :, slot * LANES : (slot + 1) * LANES]
+            back_ref[quad * tiles + tile, slot * QUAD : (slot + 1) * QUAD]
             for quad in range(cells_y // QUAD)
         ],
         axis=0,
@@ -296,31 +311,37 @@
     edges_ref,
     sent_ref,
     left_ref,
+    near_ref,
 ):
     cells_x, cells_y, velocities = reach_ref.shape
     tiles = velocities // LANES
     cells = cells_x * cells_y
-    half = left_ref.shape[0] // 2
     me = lax.axis_index("gx")
     from_left = jnp.where(me > 0, 1.0, 0.0)
     from_right = jnp.where(me < slabs - 1, 1.0, 0.0)
 
     def put(row, value, lanes):
-        high = value.astype(jnp.bfloat16)
-        low = (value - high.astype(jnp.float32)).astype(jnp.bfloat16)
-        left_ref[row : row + cells_y, lanes] = high
-        left_ref[half + row : half + row + cells_y, lanes] = low
-
+        split_put(left_ref, row, lanes, value)
+
+    near_ref[...] = jnp.zeros_like(near_ref)
+    for n, k in enumerate(EDGE_ROWS):
+        row = 1 + n // QUAD
+        start = (n % QUAD) * 2 * cells_y
+        near_ref[k : k + 1, 0:cells_y] = (
+            edges_ref[row : row + 1, start + cells_y : start + 2 * cells_y] * from_left
+        )
+        near_ref[k : k + 1, cells_y : 2 * cells_y] = (
+            edges_ref[QUAD + row : QUAD + row + 1, start : start + cells_y] * from_right
+        )
     columns = edges_ref[...].T
     relax_left = jnp.broadcast_to(columns[cells - cells_y : cells, 0:1], (cells_y, LANES))
-    relax_right = jnp.broadcast_to(columns[0:cells_y, 1:2], (cells_y, LANES))
+    relax_right = jnp.broadcast_to(columns[0:cells_y, QUAD : QUAD + 1], (cells_y, LANES))
     for tile in range(tiles):
         lanes = slice(tile * LANES, (tile + 1) * LANES)
         forward = jnp.broadcast_to(table_ref[0:1, lanes], (cells_y, LANES)) > 0.5
         courant = jnp.broadcast_to(table_ref[1:2, lanes], (cells_y, LANES))
         entry = whole_rows(back_ref, 0, tile, tiles, cells_y)
         mixed = whole_rows(back_ref, 1, tile, tiles, cells_y)
-        gain = whole_rows(back_ref, 2, tile, tiles, cells_y)
         answer = jnp.where(forward, mixed, 0.0)
         leaving = jnp.where(forward, 0.0, mixed)
         for x in range(cells_x):
@@ -335,7 +356,7 @@
                 outgoing_answer = reach * answer
         decay = courant / (1.0 + courant + jnp.where(forward, relax_right, relax_left))
         inside = jnp.where(forward, from_right, from_left)
-        near = (decay * outgoing + gain) * inside
+        near = decay * outgoing * inside
         near_answer = decay * outgoing_answer * inside
         row = 2 * cells
         put(row, jnp.where(forward, entry * from_left, near), lanes)
@@ -347,17 +368,10 @@
         put(row + 6 * cells_y, jnp.zeros_like(entry), lanes)
         put(row + 7 * cells_y, jnp.zeros_like(entry), lanes)
 
-    product = lax.dot_general(
-        psi_ref[...],
-        left_ref[...],
-        (((1,), (1,)), ((), ())),
-        preferred_element_type=jnp.float32,
-    )
-    upper = product[:, 0:half]
-    total = upper[0:16] + upper[16:32] + product[0:16, half:]
+    total = split_moments(psi_ref, left_ref)
     fixed = total[:, 0:cells]
     answer = total[:, cells : 2 * cells]
-    edges = total[:, 2 * cells : 3 * cells]
+    edges = total[:, 2 * cells : 3 * cells] + near_ref[...]
 
     spread = line_ref[2:3, :]
     lane = lax.broadcasted_iota(jnp.int32, (16, cells), 1)
@@ -536,7 +550,7 @@
         (
             near(state.shape, f32),
             near(state.shape, f32),
-            near((slabs, 2, (QUAD + 1) * LANES), f32),
+            near((slabs, 2 * QUAD, LANES), f32),
             near((slabs, 4 * QUAD, LANES), f32),
             near((32, velocities), jnp.bfloat16),
             near((32, velocities), jnp.bfloat16),
@@ -550,6 +564,8 @@
             pltpu.VMEM((16, velocities), f32),
             pltpu.VMEM((cells, velocities), f32),
             pltpu.VMEM((cells_x + 1, cells_y, LANES), f32),
+            pltpu.VMEM((8 * cells_y, velocities), jnp.bfloat16),
+            pltpu.VMEM((8, LANES), f32),
             pltpu.SemaphoreType.DMA((cells_y // 8 + 7,)),
         ],
         *sources,
@@ -560,8 +576,8 @@
     maps = held(lax.all_to_all(sent, "gx", 0, 0))
     entries, edges = call(
         lambda *refs: scan_kernel(cells_x, *refs),
-        (near((slabs, QUAD, 3 * LANES), f32), near((8, LANES), f32)),
-        [pltpu.VMEM((slabs, QUAD, LANES), f32)] * 3,
+        (near((slabs, 2 * QUAD, LANES), f32), near((8, LANES), f32)),
+        [pltpu.VMEM((slabs, QUAD, LANES), f32)] * 2,
         maps,
         side,
     )
@@ -570,7 +586,10 @@
     partial_sums = call(
         lambda *refs: moments_kernel(groups, slabs, *refs),
         near((groups, QUAD, SENT_PARTS * cells), f32),
-        [pltpu.VMEM((6 * cells, velocities), jnp.bfloat16)],
+        [
+            pltpu.VMEM((6 * cells, velocities), jnp.bfloat16),
+            pltpu.VMEM((16, cells), f32),
+        ],
         reach,
         run,
         back,

time: 64.9 us -> 64.3 us (level)
  blocking collectives: 59.4 us -> 58.5 us
where the time goes in v6:
time: 64.3 us; the launch traced here: 64.1 us
  blocking collectives  58.5 us (91%)
  Pallas kernels  4.96 us (8%)
  between operations  0.66 us (1%)
    all_to_all x1, blocking collectives, local(): parts = held(lax.all_to_all(partial_sums, 'vert', 0, 0))  32.3 us
    all_to_all x1, blocking collectives, local(): maps = held(lax.all_to_all(sent, 'gx', 0, 0))  14.9 us
    all_to_all x1, blocking collectives, local(): back = held(lax.all_to_all(entries, 'gx', 0, 0))  11.2 us
    pallas_call x4, Pallas kernels, call(): pl.pallas_call(body, out_shape=outs, scratch_shapes=scratch, interpret=IN...  4.96 us

profile of v6, /device:TPU:32, one launch (start us, length us, event | category | flops | bytes accessed | tf_op | source)
XLA Modules:
  0.0 64.1 jit_solution(7073050691773527909)
XLA Ops:
  0.6 2.2 %shard_map.95 = (f32[8,16,1024]{2,1,0:T(8,128)S(1)}, f32[8,16,1024]{2,1,0:T(8,128)S(1)}, f32[32,8,128]{2,1,0:T(8,128)S(1)}, f32[32,16,128]{2,1,0:T(8,128)S(1)}, ...) custom-call(f32[8,16,1024]{2,1,0:T(8,128)} %refs_0_.1, ...), custom_call_target="tpu_custom_call" | custom-call | tf_op jit(solution)/shard_map/pallas_call | solution.py:542
  2.8 14.9 %all_to_all.15.refs_0_ = f32[32,8,128]{2,1,0:T(8,128)S(1)} all-to-all(f32[32,8,128]{2,1,0:T(8,128)S(1)} %get-tuple-element.14), channel_id=1, replica_groups=mesh['gx'=32,'vert'=16] {'gx'}, dimensions={0} | all-to-all | bytes 262144 | tf_op jit(solution)/shard_map/all_to_all | solution.py:576
  17.7 0.5 shard_map.96
  18.2 11.2 %all_to_all.16.refs_2_.back_ref = f32[32,8,128]{2,1,0:T(8,128)S(1)} all-to-all(f32[32,8,128]{2,1,0:T(8,128)S(1)} %get-tuple-element.16), channel_id=1, replica_groups=mesh['gx'=32,'vert'=16] {'gx'}, dimensions={0} | all-to-all | bytes 262144 | tf_op jit(solution)/shard_map/all_to_all | solution.py:585
  29.4 0.8 %shard_map.97 = f32[16,4,896]{2,1,0:T(4,128)S(1)} custom-call(f32[8,16,1024]{2,1,0:T(8,128)S(1)} %get-tuple-element.12.refs_0_.reach_ref, f32[8,16,1024]{2,1,0:T(8,128)S(1)} %get-tuple-element.13.refs_1_.run_ref, f32[32,8,128]{2,1,0:T(8,128)S(1)} %all_to_all.16.refs_2_.back_ref, bf16[32,1024]{1,0:T(8,128)(2,1)S(1)} %get-tuple-element.17.refs_3_, ...), custom_call_target="tpu_custom_call" | custom-call | tf_op jit(solution)/shard_map/pallas_call | solution.py:542
  30.3 32.3 %all_to_all.17.parts_ref = f32[16,4,896]{2,1,0:T(4,128)S(1)} all-to-all(f32[16,4,896]{2,1,0:T(4,128)S(1)} %shard_map.97), channel_id=1, replica_groups=mesh['gx'=32,'vert'=16] {'vert'}, dimensions={0} | all-to-all | bytes 458752 | tf_op jit(solution)/shard_map/all_to_all | solution.py:601
  62.6 1.5 %shard_map.98 = (f32[8,16,1024]{2,1,0:T(8,128)}, f32[5,8,16]{2,1,0:T(8,128)}) custom-call(f32[16,4,896]{2,1,0:T(4,128)S(1)} %all_to_all.17.parts_ref, f32[8,16,1024]{2,1,0:T(8,128)S(1)} %get-tuple-element.12.refs_0_.reach_ref, f32[8,16,1024]{2,1,0:T(8,128)S(1)} %get-tuple-element.13.refs_1_.run_ref, f32[32,8,128]{2,1,0:T(8,128)S(1)} %all_to_all.16.refs_2_.back_ref, ...), custom_call_target="tpu_custom_call" | custom-call | tf_op jit(solution)/shard_map/pallas_call | solution.py:542

commit v7 on v6

--- a/solution.py
+++ b/solution.py
@@ -86,6 +86,7 @@
     equil_ref,
     spread_ref,
     left_ref,
+    right_ref,
     message_ref,
     sems,
 ):
@@ -117,7 +118,7 @@
     ]
     for copy in large + small:
         copy.start()
-    for ref in (cells_ref, basis_ref, moment_ref, table_ref, line_ref, message_ref, left_ref):
+    for ref in (cells_ref, basis_ref, moment_ref, table_ref, line_ref, message_ref):
         ref[...] = jnp.zeros_like(ref)
     for copy in small:
         copy.wait()
@@ -134,6 +135,7 @@
     spread_ref[cells_x] = jnp.broadcast_to(columns[0:cells_y, 1:2], (cells_y, LANES))
     relax_row = line_ref[0:1, :]
     line_ref[2:3, :] = 0.2 / (1.0 + relax_row)
+    message_ref[0:1, :] = relax_row
 
     magnitude = velocity_ref[0:1, :]
     positive = sign_ref[...] == 1
@@ -174,8 +176,9 @@
     psi_ref[16:32] = (moment_ref[...] - high.astype(jnp.float32)).astype(jnp.bfloat16)
 
     last = cells_x - 1
+    large[0].wait()
     for half in range(halves):
-        large[half].wait()
+        edge_ref = (left_ref, right_ref)[half]
         rows = slice(half * 8, half * 8 + 8)
         for tile in range(tiles):
             lanes = slice(tile * LANES, (tile + 1) * LANES)
@@ -208,22 +211,21 @@
             direction = jnp.where(forward, 1.0, 0.0)
             first_gain = gains[0]
             outward = jnp.where(forward, first_gain, 0.0)
-            split_put(left_ref, half * 8, lanes, outward)
-            split_put(left_ref, cells_y + half * 8, lanes, first_gain - outward)
+            split_put(edge_ref, 0, lanes, outward)
+            split_put(edge_ref, 8, lanes, first_gain - outward)
             for part in range(8 // QUAD):
                 owner = (half * (8 // QUAD) + part) * tiles + tile
                 quad = slice(part * QUAD, (part + 1) * QUAD)
                 sent_ref[owner, 0:QUAD, :] = runs[last][quad]
                 for slot, value in enumerate((fixed, unit, direction, courant)):
                     side_ref[owner, slot * QUAD : (slot + 1) * QUAD, :] = value[quad]
-    message_ref[0:1, :] = relax_row
-    edge_moments = split_moments(psi_ref, left_ref)
-    for n, k in enumerate(EDGE_ROWS):
-        row = 1 + n // QUAD
-        start = (n % QUAD) * 2 * cells_y
-        message_ref[row : row + 1, start : start + 2 * cells_y] = edge_moments[
-            k : k + 1, 0 : 2 * cells_y
-        ]
+        if half + 1 < halves:
+            large[half + 1].wait()
+        edge_moments = split_moments(psi_ref, edge_ref)
+        for n, k in enumerate(EDGE_ROWS):
+            row = 1 + n // QUAD
+            start = (n % QUAD) * 2 * cells_y + half * 16
+            message_ref[row : row + 1, start : start + 16] = edge_moments[k : k + 1, :]
     message = message_ref[0:QUAD]
     for owner in range(sent_ref.shape[0]):
         sent_ref[owner, QUAD : 2 * QUAD, :] = message
@@ -324,14 +326,21 @@
         split_put(left_ref, row, lanes, value)
 
     near_ref[...] = jnp.zeros_like(near_ref)
+    tile = edges_ref[...]
+    place = lax.broadcasted_iota(jnp.int32, tile.shape, 1) % (2 * cells_y) // 8
+    tile = jnp.where(
+        place == 1,
+        pltpu.roll(tile, cells - 8, 1),
+        jnp.where(place == 2, pltpu.roll(tile, 8, 1), tile),
+    )
     for n, k in enumerate(EDGE_ROWS):
         row = 1 + n // QUAD
         start = (n % QUAD) * 2 * cells_y
         near_ref[k : k + 1, 0:cells_y] = (
-            edges_ref[row : row + 1, start + cells_y : start + 2 * cells_y] * from_left
+            tile[row : row + 1, start + cells_y : start + 2 * cells_y] * from_left
         )
         near_ref[k : k + 1, cells_y : 2 * cells_y] = (
-            edges_ref[QUAD + row : QUAD + row + 1, start : start + cells_y] * from_right
+            tile[QUAD + row : QUAD + row + 1, start : start + cells_y] * from_right
         )
     columns = edges_ref[...].T
     relax_left = jnp.broadcast_to(columns[cells - cells_y : cells, 0:1], (cells_y, LANES))
@@ -564,7 +573,8 @@
             pltpu.VMEM((16, velocities), f32),
             pltpu.VMEM((cells, velocities), f32),
             pltpu.VMEM((cells_x + 1, cells_y, LANES), f32),
-            pltpu.VMEM((8 * cells_y, velocities), jnp.bfloat16),
+            pltpu.VMEM((32, velocities), jnp.bfloat16),
+            pltpu.VMEM((32, velocities), jnp.bfloat16),
             pltpu.VMEM((8, LANES), f32),
             pltpu.SemaphoreType.DMA((cells_y // 8 + 7,)),
         ],

time: 64.3 us -> 64.3 us (level)
  no operation moved by 1% of the time
where the time goes in v7:
time: 64.3 us; the launch traced here: 64 us
  blocking collectives  58.5 us (91%)
  Pallas kernels  4.91 us (8%)
  between operations  0.66 us (1%)
    all_to_all x1, blocking collectives, local(): parts = held(lax.all_to_all(partial_sums, 'vert', 0, 0))  32.3 us
    all_to_all x1, blocking collectives, local(): maps = held(lax.all_to_all(sent, 'gx', 0, 0))  14.9 us
    all_to_all x1, blocking collectives, local(): back = held(lax.all_to_all(entries, 'gx', 0, 0))  11.2 us
    pallas_call x4, Pallas kernels, call(): pl.pallas_call(body, out_shape=outs, scratch_shapes=scratch, interpret=IN...  4.91 us

profile of v7, /device:TPU:32, one launch (start us, length us, event | category | flops | bytes accessed | tf_op | source)
XLA Modules:
  0.0 64.0 jit_solution(1506838061812000915)
XLA Ops:
  0.6 2.1 %shard_map.95 = (f32[8,16,1024]{2,1,0:T(8,128)S(1)}, f32[8,16,1024]{2,1,0:T(8,128)S(1)}, f32[32,8,128]{2,1,0:T(8,128)S(1)}, f32[32,16,128]{2,1,0:T(8,128)S(1)}, ...) custom-call(f32[8,16,1024]{2,1,0:T(8,128)} %refs_0_.1, ...), custom_call_target="tpu_custom_call" | custom-call | tf_op jit(solution)/shard_map/pallas_call | solution.py:551
  2.8 14.9 %all_to_all.15.refs_0_ = f32[32,8,128]{2,1,0:T(8,128)S(1)} all-to-all(f32[32,8,128]{2,1,0:T(8,128)S(1)} %get-tuple-element.14), channel_id=1, replica_groups=mesh['gx'=32,'vert'=16] {'gx'}, dimensions={0} | all-to-all | bytes 262144 | tf_op jit(solution)/shard_map/all_to_all | solution.py:586
  17.7 0.5 shard_map.96
  18.1 11.2 %all_to_all.16.refs_2_.back_ref = f32[32,8,128]{2,1,0:T(8,128)S(1)} all-to-all(f32[32,8,128]{2,1,0:T(8,128)S(1)} %get-tuple-element.16), channel_id=1, replica_groups=mesh['gx'=32,'vert'=16] {'gx'}, dimensions={0} | all-to-all | bytes 262144 | tf_op jit(solution)/shard_map/all_to_all | solution.py:595
  29.4 0.8 %shard_map.97 = f32[16,4,896]{2,1,0:T(4,128)S(1)} custom-call(f32[8,16,1024]{2,1,0:T(8,128)S(1)} %get-tuple-element.12.refs_0_.reach_ref, f32[8,16,1024]{2,1,0:T(8,128)S(1)} %get-tuple-element.13.refs_1_.run_ref, f32[32,8,128]{2,1,0:T(8,128)S(1)} %all_to_all.16.refs_2_.back_ref, bf16[32,1024]{1,0:T(8,128)(2,1)S(1)} %get-tuple-element.17.refs_3_, ...), custom_call_target="tpu_custom_call" | custom-call | tf_op jit(solution)/shard_map/pallas_call | solution.py:551
  30.2 32.3 %all_to_all.17.parts_ref = f32[16,4,896]{2,1,0:T(4,128)S(1)} all-to-all(f32[16,4,896]{2,1,0:T(4,128)S(1)} %shard_map.97), channel_id=1, replica_groups=mesh['gx'=32,'vert'=16] {'vert'}, dimensions={0} | all-to-all | bytes 458752 | tf_op jit(solution)/shard_map/all_to_all | solution.py:611
  62.5 1.5 %shard_map.98 = (f32[8,16,1024]{2,1,0:T(8,128)}, f32[5,8,16]{2,1,0:T(8,128)}) custom-call(f32[16,4,896]{2,1,0:T(4,128)S(1)} %all_to_all.17.parts_ref, f32[8,16,1024]{2,1,0:T(8,128)S(1)} %get-tuple-element.12.refs_0_.reach_ref, f32[8,16,1024]{2,1,0:T(8,128)S(1)} %get-tuple-element.13.refs_1_.run_ref, f32[32,8,128]{2,1,0:T(8,128)S(1)} %all_to_all.16.refs_2_.back_ref, ...), custom_call_target="tpu_custom_call" | custom-call | tf_op jit(solution)/shard_map/pallas_call | solution.py:551

commit v8 on v6

--- a/solution.py
+++ b/solution.py
@@ -86,6 +86,8 @@
     equil_ref,
     spread_ref,
     left_ref,
+    edge_decay_ref,
+    edge_driven_ref,
     message_ref,
     sems,
 ):
@@ -93,8 +95,15 @@
     velocities = state_ref.shape[2]
     tiles = velocities // LANES
     halves = cells_y // 8
+    last = cells_x - 1
+    large = [
+        pltpu.make_async_copy(
+            state_hbm.at[pl.ds(start, count)], state_ref.at[pl.ds(start, count)], sems.at[n]
+        )
+        for n, (start, count) in enumerate(((0, 1), (last, 1), (1, cells_x - 2)))
+    ]
     small = [
-        pltpu.make_async_copy(source, target, sems.at[halves + n])
+        pltpu.make_async_copy(source, target, sems.at[len(large) + n])
         for n, (source, target) in enumerate(
             (
                 (velocity_hbm, velocity_ref),
@@ -107,17 +116,9 @@
             )
         )
     ]
-    large = [
-        pltpu.make_async_copy(
-            state_hbm.at[:, pl.ds(half * 8, 8), :],
-            state_ref.at[:, pl.ds(half * 8, 8), :],
-            sems.at[half],
-        )
-        for half in range(halves)
-    ]
-    for copy in large + small:
+    for copy in large[0:2] + small + large[2:]:
         copy.start()
-    for ref in (cells_ref, basis_ref, moment_ref, table_ref, line_ref, message_ref, left_ref):
+    for ref in (cells_ref, basis_ref, moment_ref, table_ref, line_ref, message_ref):
         ref[...] = jnp.zeros_like(ref)
     for copy in small:
         copy.wait()
@@ -134,6 +135,7 @@
     spread_ref[cells_x] = jnp.broadcast_to(columns[0:cells_y, 1:2], (cells_y, LANES))
     relax_row = line_ref[0:1, :]
     line_ref[2:3, :] = 0.2 / (1.0 + relax_row)
+    message_ref[0:1, :] = relax_row
 
     magnitude = velocity_ref[0:1, :]
     positive = sign_ref[...] == 1
@@ -173,24 +175,49 @@
     psi_ref[0:16] = high
     psi_ref[16:32] = (moment_ref[...] - high.astype(jnp.float32)).astype(jnp.bfloat16)
 
-    last = cells_x - 1
+    def cell(x, rows, lanes, courant):
+        relax = spread_ref[x, rows]
+        first = x * cells_y + rows.start
+        inverse = 1.0 / (1.0 + courant + relax)
+        gain = state_ref[x, rows, lanes] + relax * equil_ref[first : first + 8, lanes]
+        return courant * inverse, gain * inverse
+
+    def settings(lanes):
+        forward = jnp.broadcast_to(table_ref[0:1, lanes], (8, LANES)) > 0.5
+        return forward, jnp.broadcast_to(table_ref[1:2, lanes], (8, LANES))
+
+    for copy in large[0:2]:
+        copy.wait()
     for half in range(halves):
-        large[half].wait()
         rows = slice(half * 8, half * 8 + 8)
         for tile in range(tiles):
             lanes = slice(tile * LANES, (tile + 1) * LANES)
-            forward = jnp.broadcast_to(table_ref[0:1, lanes], (8, LANES)) > 0.5
-            courant = jnp.broadcast_to(table_ref[1:2, lanes], (8, LANES))
-            base = 1.0 + courant
-            decay = []
-            driven = []
-            for x in range(cells_x):
-                relax = spread_ref[x, rows]
-                first = x * cells_y + half * 8
-                equil = equil_ref[first : first + 8, lanes]
-                inverse = 1.0 / (base + relax)
-                decay.append(courant * inverse)
-                driven.append((state_ref[x, rows, lanes] + relax * equil) * inverse)
+            forward, courant = settings(lanes)
+            pair = [cell(x, rows, lanes, courant) for x in (0, last)]
+            for n in range(2):
+                edge_decay_ref[n, rows, lanes] = pair[n][0]
+                edge_driven_ref[n, rows, lanes] = pair[n][1]
+            split_put(left_ref, half * 8, lanes, jnp.where(forward, pair[0][1], 0.0))
+            split_put(left_ref, cells_y + half * 8, lanes, jnp.where(forward, 0.0, pair[1][1]))
+    large[2].wait()
+    edge_moments = split_moments(psi_ref, left_ref)
+    for n, k in enumerate(EDGE_ROWS):
+        row = 1 + n // QUAD
+        start = (n % QUAD) * 2 * cells_y
+        message_ref[row : row + 1, start : start + 2 * cells_y] = edge_moments[k : k + 1, :]
+    for half in range(halves):
+        rows = slice(half * 8, half * 8 + 8)
+        for tile in range(tiles):
+            lanes = slice(tile * LANES, (tile + 1) * LANES)
+            forward, courant = settings(lanes)
+            decay = [edge_decay_ref[0, rows, lanes]]
+            driven = [edge_driven_ref[0, rows, lanes]]
+            for x in range(1, last):
+                one, two = cell(x, rows, lanes, courant)
+                decay.append(one)
+                driven.append(two)
+            decay.append(edge_decay_ref[1, rows, lanes])
+            driven.append(edge_driven_ref[1, rows, lanes])
             steps = [jnp.where(forward, decay[t], decay[last - t]) for t in range(cells_x)]
             gains = [jnp.where(forward, driven[t], driven[last - t]) for t in range(cells_x)]
             products = [steps[0]]
@@ -206,24 +233,12 @@
             fixed = jnp.where(diffuse, 0.0, free_ref[rows, lanes])
             unit = jnp.where(diffuse, 1.0, 0.0)
             direction = jnp.where(forward, 1.0, 0.0)
-            first_gain = gains[0]
-            outward = jnp.where(forward, first_gain, 0.0)
-            split_put(left_ref, half * 8, lanes, outward)
-            split_put(left_ref, cells_y + half * 8, lanes, first_gain - outward)
             for part in range(8 // QUAD):
                 owner = (half * (8 // QUAD) + part) * tiles + tile
                 quad = slice(part * QUAD, (part + 1) * QUAD)
                 sent_ref[owner, 0:QUAD, :] = runs[last][quad]
                 for slot, value in enumerate((fixed, unit, direction, courant)):
                     side_ref[owner, slot * QUAD : (slot + 1) * QUAD, :] = value[quad]
-    message_ref[0:1, :] = relax_row
-    edge_moments = split_moments(psi_ref, left_ref)
-    for n, k in enumerate(EDGE_ROWS):
-        row = 1 + n // QUAD
-        start = (n % QUAD) * 2 * cells_y
-        message_ref[row : row + 1, start : start + 2 * cells_y] = edge_moments[
-            k : k + 1, 0 : 2 * cells_y
-        ]
     message = message_ref[0:QUAD]
     for owner in range(sent_ref.shape[0]):
         sent_ref[owner, QUAD : 2 * QUAD, :] = message
@@ -564,9 +579,11 @@
             pltpu.VMEM((16, velocities), f32),
             pltpu.VMEM((cells, velocities), f32),
             pltpu.VMEM((cells_x + 1, cells_y, LANES), f32),
-            pltpu.VMEM((8 * cells_y, velocities), jnp.bfloat16),
+            pltpu.VMEM((4 * cells_y, velocities), jnp.bfloat16),
+            pltpu.VMEM((2, cells_y, velocities), f32),
+            pltpu.VMEM((2, cells_y, velocities), f32),
             pltpu.VMEM((8, LANES), f32),
-            pltpu.SemaphoreType.DMA((cells_y // 8 + 7,)),
+            pltpu.SemaphoreType.DMA((10,)),
         ],
         *sources,
         in_specs=[anywhere] * len(sources),

time: 64.3 us -> 64.2 us (level)
  no operation moved by 1% of the time
where the time goes in v8:
time: 64.2 us; the launch traced here: 64 us
  blocking collectives  58.4 us (91%)
  Pallas kernels  4.88 us (8%)
  between operations  0.66 us (1%)
    all_to_all x1, blocking collectives, local(): parts = held(lax.all_to_all(partial_sums, 'vert', 0, 0))  32.3 us
    all_to_all x1, blocking collectives, local(): maps = held(lax.all_to_all(sent, 'gx', 0, 0))  14.9 us
    all_to_all x1, blocking collectives, local(): back = held(lax.all_to_all(entries, 'gx', 0, 0))  11.2 us
    pallas_call x4, Pallas kernels, call(): pl.pallas_call(body, out_shape=outs, scratch_shapes=scratch, interpret=IN...  4.88 us

profile of v8, /device:TPU:32, one launch (start us, length us, event | category | flops | bytes accessed | tf_op | source)
XLA Modules:
  0.0 64.0 jit_solution(16324453654368690008)
XLA Ops:
  0.6 2.1 %shard_map.95 = (f32[8,16,1024]{2,1,0:T(8,128)S(1)}, f32[8,16,1024]{2,1,0:T(8,128)S(1)}, f32[32,8,128]{2,1,0:T(8,128)S(1)}, f32[32,16,128]{2,1,0:T(8,128)S(1)}, ...) custom-call(f32[8,16,1024]{2,1,0:T(8,128)} %refs_0_.1, ...), custom_call_target="tpu_custom_call" | custom-call | tf_op jit(solution)/shard_map/pallas_call | solution.py:557
  2.7 14.9 %all_to_all.15.refs_0_ = f32[32,8,128]{2,1,0:T(8,128)S(1)} all-to-all(f32[32,8,128]{2,1,0:T(8,128)S(1)} %get-tuple-element.14), channel_id=1, replica_groups=mesh['gx'=32,'vert'=16] {'gx'}, dimensions={0} | all-to-all | bytes 262144 | tf_op jit(solution)/shard_map/all_to_all | solution.py:593
  17.6 0.5 shard_map.96
  18.1 11.2 %all_to_all.16.refs_2_.back_ref = f32[32,8,128]{2,1,0:T(8,128)S(1)} all-to-all(f32[32,8,128]{2,1,0:T(8,128)S(1)} %get-tuple-element.16), channel_id=1, replica_groups=mesh['gx'=32,'vert'=16] {'gx'}, dimensions={0} | all-to-all | bytes 262144 | tf_op jit(solution)/shard_map/all_to_all | solution.py:602
  29.4 0.8 %shard_map.97 = f32[16,4,896]{2,1,0:T(4,128)S(1)} custom-call(f32[8,16,1024]{2,1,0:T(8,128)S(1)} %get-tuple-element.12.refs_0_.reach_ref, f32[8,16,1024]{2,1,0:T(8,128)S(1)} %get-tuple-element.13.refs_1_.run_ref, f32[32,8,128]{2,1,0:T(8,128)S(1)} %all_to_all.16.refs_2_.back_ref, bf16[32,1024]{1,0:T(8,128)(2,1)S(1)} %get-tuple-element.17.refs_3_, ...), custom_call_target="tpu_custom_call" | custom-call | tf_op jit(solution)/shard_map/pallas_call | solution.py:557
  30.2 32.3 %all_to_all.17.parts_ref = f32[16,4,896]{2,1,0:T(4,128)S(1)} all-to-all(f32[16,4,896]{2,1,0:T(4,128)S(1)} %shard_map.97), channel_id=1, replica_groups=mesh['gx'=32,'vert'=16] {'vert'}, dimensions={0} | all-to-all | bytes 458752 | tf_op jit(solution)/shard_map/all_to_all | solution.py:618
  62.5 1.5 %shard_map.98 = (f32[8,16,1024]{2,1,0:T(8,128)}, f32[5,8,16]{2,1,0:T(8,128)}) custom-call(f32[16,4,896]{2,1,0:T(4,128)S(1)} %all_to_all.17.parts_ref, f32[8,16,1024]{2,1,0:T(8,128)S(1)} %get-tuple-element.12.refs_0_.reach_ref, f32[8,16,1024]{2,1,0:T(8,128)S(1)} %get-tuple-element.13.refs_1_.run_ref, f32[32,8,128]{2,1,0:T(8,128)S(1)} %all_to_all.16.refs_2_.back_ref, ...), custom_call_target="tpu_custom_call" | custom-call | tf_op jit(solution)/shard_map/pallas_call | solution.py:557

commit v9 on v8

--- a/solution.py
+++ b/solution.py
@@ -8,7 +8,6 @@
 LANES = 128
 QUAD = 4
 EDGE_ROWS = (0, 1, 2, 3, 4, 5, 6, 8, 10)
-SENT_PARTS = 7
 INTERPRET = False
 
 
@@ -429,26 +428,29 @@
     change = spread * (laplace + laplace_across) - 0.25 * (flow + flow_across)
     laplace, flow = along(answer, placed[2], placed[3])
     change_answer = spread * laplace - 0.25 * flow
-    message = [
-        fixed[0:5],
-        change,
-        answer[0:5],
-        answer[5:6],
-        answer[7:8],
-        answer[9:10],
-        answer[11:12],
-        change_answer,
-        edges[13:14],
-    ]
-    spare = QUAD * (sent_ref.shape[2] // cells) - 25
-    message = jnp.concatenate(message + [jnp.zeros((spare, cells), jnp.float32)], axis=0)
-    for part in range(sent_ref.shape[2] // cells):
-        piece = message[part * QUAD : (part + 1) * QUAD]
-        for group in range(groups):
-            sent_ref[group, :, part * cells : (part + 1) * cells] = piece
+    lane = lax.broadcasted_iota(jnp.int32, (1, cells), 1)
+    final = jnp.where(
+        lane < 6 * cells_y, edges[13:14], pltpu.roll(answer[5:6], 6 * cells_y, 1)
+    )
+    message = jnp.concatenate(
+        [
+            fixed[0:5],
+            change,
+            answer[0:5],
+            answer[7:8],
+            answer[9:10],
+            answer[11:12],
+            change_answer,
+            final,
+        ],
+        axis=0,
+    )
+    for group in range(groups):
+        sent_ref[group] = message
 
 
 def finish_kernel(
+    total_cells,
     parts_ref,
     reach_ref,
     run_ref,
@@ -471,34 +473,37 @@
     sums = [parts_ref[group] for group in range(groups)]
     while len(sums) > 1:
         sums = [sums[n] + sums[n + 1] for n in range(0, len(sums), 2)]
-    total = jnp.concatenate(
-        [sums[0][:, n * cells : (n + 1) * cells] for n in range(parts_ref.shape[2] // cells)],
-        axis=0,
-    )
+    total = sums[0]
     lane = lax.broadcasted_iota(jnp.int32, (1, cells), 1)
-    sums = total[24:25]
+    sums = total[23:24]
     here = jnp.logical_and(lane >= 4 * cells_y, lane < 5 * cells_y)
     incoming = jnp.where(here, pltpu.roll(sums, cells - cells_y, 1), 1.0)
     rho = jnp.where(here, sums, 0.0) / incoming
+    start = jnp.logical_and(lane >= 6 * cells_y, lane < 7 * cells_y)
+    across_flow = jnp.where(start, sums, 0.0)
+    lost = jnp.where(lane >= cells_y, (1.0 + line_ref[0:1, :]) * total[12:13], 0.0)
     width = cells_y
     while width < cells:
         rho = rho + pltpu.roll(rho, width, 1)
+        across_flow = across_flow + pltpu.roll(across_flow, width, 1)
+        lost = lost + jnp.where(lane >= width, pltpu.roll(lost, width, 1), 0.0)
         width *= 2
-    answer = rho * total[8:24]
+    across_flow = across_flow - (2.0 / total_cells) * lost
+    answer = rho * jnp.concatenate([total[8:23], across_flow], axis=0)
     yp, ym = across_neighbours(answer, cells_y)
     dy = yp - ym
     flow = jnp.concatenate(
         [
             dy[4:5],
+            dy[15:16],
+            dy[2:3] + dy[6:7] + dy[8:9],
             dy[7:8],
-            dy[2:3] + dy[6:7] + dy[9:10],
-            dy[8:9],
-            2.0 / 3.0 * (dy[4:5] + dy[10:11]),
+            2.0 / 3.0 * (dy[4:5] + dy[9:10]),
         ],
         axis=0,
     )
     spread = line_ref[2:3, :]
-    change = total[5:10] + rho * total[19:24] + spread * (yp + ym)[2:7] - 0.25 * flow
+    change = total[5:10] + rho * total[18:23] + spread * (yp + ym)[2:7] - 0.25 * flow
     updated = total[0:5] + answer[2:7] + change
     for x in range(cells_x):
         macro_ref[:, x, :] = updated[:, x * cells_y : (x + 1) * cells_y]
@@ -602,7 +607,7 @@
     back = held(lax.all_to_all(entries, "gx", 0, 0))
     partial_sums = call(
         lambda *refs: moments_kernel(groups, slabs, *refs),
-        near((groups, QUAD, SENT_PARTS * cells), f32),
+        near((groups, 24, cells), f32),
         [
             pltpu.VMEM((6 * cells, velocities), jnp.bfloat16),
             pltpu.VMEM((16, cells), f32),
@@ -617,7 +622,7 @@
     )
     parts = held(lax.all_to_all(partial_sums, "vert", 0, 0))
     new_state, new_macro = call(
-        finish_kernel,
+        lambda *refs: finish_kernel(float(cells_x * slabs), *refs),
         (shape(state.shape, f32), shape(macro.shape, f32)),
         [
             pltpu.VMEM(state.shape, f32),

time: 64.2 us -> 63.1 us (0.983)
  blocking collectives: 58.4 us -> 57.3 us
    all_to_all x1, blocking collectives: 32.3 us -> 31.2 us  [local(): parts = held(lax.all_to_all(partial_sums, 'vert', 0, 0))]
where the time goes in v9:
time: 63.1 us; the launch traced here: 62.9 us
  blocking collectives  57.3 us (91%)
  Pallas kernels  4.88 us (8%)
  between operations  0.66 us (1%)
    all_to_all x1, blocking collectives, local(): parts = held(lax.all_to_all(partial_sums, 'vert', 0, 0))  31.2 us
    all_to_all x1, blocking collectives, local(): maps = held(lax.all_to_all(sent, 'gx', 0, 0))  14.9 us
    all_to_all x1, blocking collectives, local(): back = held(lax.all_to_all(entries, 'gx', 0, 0))  11.2 us
    pallas_call x4, Pallas kernels, call(): pl.pallas_call(body, out_shape=outs, scratch_shapes=scratch, interpret=IN...  4.88 us

profile of v9, /device:TPU:32, one launch (start us, length us, event | category | flops | bytes accessed | tf_op | source)
XLA Modules:
  0.0 62.9 jit_solution(7285386538019776315)
XLA Ops:
  0.6 2.1 %shard_map.95 = (f32[8,16,1024]{2,1,0:T(8,128)S(1)}, f32[8,16,1024]{2,1,0:T(8,128)S(1)}, f32[32,8,128]{2,1,0:T(8,128)S(1)}, f32[32,16,128]{2,1,0:T(8,128)S(1)}, ...) custom-call(f32[8,16,1024]{2,1,0:T(8,128)} %refs_0_.1, ...), custom_call_target="tpu_custom_call" | custom-call | tf_op jit(solution)/shard_map/pallas_call | solution.py:562
  2.7 14.9 %all_to_all.15.refs_0_ = f32[32,8,128]{2,1,0:T(8,128)S(1)} all-to-all(f32[32,8,128]{2,1,0:T(8,128)S(1)} %get-tuple-element.14), channel_id=1, replica_groups=mesh['gx'=32,'vert'=16] {'gx'}, dimensions={0} | all-to-all | bytes 262144 | tf_op jit(solution)/shard_map/all_to_all | solution.py:598
  17.6 0.5 shard_map.96
  18.1 11.2 %all_to_all.16.refs_2_.refs_3_ = f32[32,8,128]{2,1,0:T(8,128)S(1)} all-to-all(f32[32,8,128]{2,1,0:T(8,128)S(1)} %get-tuple-element.16), channel_id=1, replica_groups=mesh['gx'=32,'vert'=16] {'gx'}, dimensions={0} | all-to-all | bytes 262144 | tf_op jit(solution)/shard_map/all_to_all | solution.py:607
  29.4 0.8 %shard_map.97 = f32[16,24,128]{2,1,0:T(8,128)S(1)} custom-call(f32[8,16,1024]{2,1,0:T(8,128)S(1)} %get-tuple-element.12.refs_0_.refs_1_, f32[8,16,1024]{2,1,0:T(8,128)S(1)} %get-tuple-element.13.refs_1_.refs_2_, f32[32,8,128]{2,1,0:T(8,128)S(1)} %all_to_all.16.refs_2_.refs_3_, bf16[32,1024]{1,0:T(8,128)(2,1)S(1)} %get-tuple-element.17.refs_3_, ...), custom_call_target="tpu_custom_call" | custom-call | tf_op jit(solution)/shard_map/pallas_call | solution.py:562
  30.2 31.2 %all_to_all.17.refs_0_ = f32[16,24,128]{2,1,0:T(8,128)S(1)} all-to-all(f32[16,24,128]{2,1,0:T(8,128)S(1)} %shard_map.97), channel_id=1, replica_groups=mesh['gx'=32,'vert'=16] {'vert'}, dimensions={0} | all-to-all | bytes 393216 | tf_op jit(solution)/shard_map/all_to_all | solution.py:623
  61.4 1.5 %shard_map.98 = (f32[8,16,1024]{2,1,0:T(8,128)}, f32[5,8,16]{2,1,0:T(8,128)}) custom-call(f32[16,24,128]{2,1,0:T(8,128)S(1)} %all_to_all.17.refs_0_, f32[8,16,1024]{2,1,0:T(8,128)S(1)} %get-tuple-element.12.refs_0_.refs_1_, f32[8,16,1024]{2,1,0:T(8,128)S(1)} %get-tuple-element.13.refs_1_.refs_2_, f32[32,8,128]{2,1,0:T(8,128)S(1)} %all_to_all.16.refs_2_.refs_3_, ...), custom_call_target="tpu_custom_call" | custom-call | tf_op jit(solution)/shard_map/pallas_call | solution.py:562
